TPU v7x, 256 devices: a whole 4x4x8 slice. The times are simulated.
256 devices in a mesh: event: 8 (over x, core), pack: 8 (over z), tensor: 4 (over y).
Axes of the slice: x: 4, y: 4, z: 8, core: 2. Of those that a mesh axis runs over, the one named last changes fastest.
Arguments:
- features: bfloat16 [32768, 1024], P(('event', 'pack', 'tensor')), may hold values from -24 to 24
- dest_owner: int32 [32768], P(('event', 'pack', 'tensor')), may hold values from 0 to 63, as said below
- dest_slot: int32 [32768], P(('event', 'pack', 'tensor')), may hold values from 0 to 127, as said below
- doc_ids: int32 [64, 512], P(('event', 'pack')), may hold values from 0 to 7, never falling along the last dimension, each value on 1 to 128 neighbouring positions
- enc_weight: bfloat16 [2, 1024, 1024], replicated, may hold values from -0.1875 to 0.1875
- attn_in: bfloat16 [4, 1024, 1024], P(None, None, 'tensor'), may hold values from -0.1875 to 0.1875
- attn_out: bfloat16 [1024, 1024], P('tensor'), may hold values from -0.1875 to 0.1875
- ffn_in: bfloat16 [2, 1024, 2048], P(None, None, 'tensor'), may hold values from -0.1875 to 0.1875
- ffn_out: bfloat16 [2048, 1024], P('tensor'), may hold values from -0.125 to 0.125
- out_grad: bfloat16 [64, 512, 1024], P(('event', 'pack'), 'tensor'), may hold values from -6 to 6
Outputs:
- packed_out: bfloat16 [64, 512, 1024], P(('event', 'pack'), 'tensor')
- row_grad: bfloat16 [32768, 1024], P(('event', 'pack', 'tensor'))
- enc_grad: float32 [2, 1024, 1024], P(None, ('event', 'pack'), 'tensor')
Inputs may be any that keep to these rules, and one draw needn't show every extreme that they name: `dest_owner`: the sequence of each event, numbered over event and pack with event slowest. From the devices of one tensor index every sequence receives exactly 128 events; from one device at most 3 events go to one sequence, every device sends exactly 3 to some sequence, and every sequence receives exactly 3 from some device. `dest_slot`: events of one tensor index that go to one sequence have distinct slots, so they fill that sequence's positions tix * 128 to tix * 128 + 127. `doc_ids`: document numbers never fall along a sequence; a document holds 1 to 128 positions.
All inputs are finite; a program needn't handle non-finite values.
Results may differ from a plain program's by a relative error of at most 0.023.
Values may be sent and summed in bfloat16 or wider, within the bound.
A program may use at most 128 MiB of HBM per device.

v0:
```python
import jax
import jax.numpy as jnp
from jax import lax
from jax.sharding import PartitionSpec as P

D = 1024
HEADS = 16


EPS = 1e-06
BLOCK = 256


def joined_along(blocks, dim):
    blocks = jnp.moveaxis(blocks, 0, dim)
    lengths = blocks.shape
    return blocks.reshape(*lengths[:dim], lengths[dim] * lengths[dim + 1], *lengths[dim + 2 :])


def sent_to_all(array, axis):
    copies = jnp.broadcast_to(array, (lax.axis_size(axis), *array.shape))
    return lax.all_to_all(copies, axis, split_axis=0, concat_axis=0, tiled=True)


def gather_directly(array, axis, dim):
    return joined_along(sent_to_all(array, axis), dim)


def cut_along(array, dim, length):
    lengths = array.shape
    blocks = array.reshape(*lengths[:dim], length, lengths[dim] // length, *lengths[dim + 1 :])
    return jnp.moveaxis(blocks, dim, 0)


def sent_and_summed(array, axis, dim):
    blocks = cut_along(array, dim, lax.axis_size(axis))
    arrived = lax.all_to_all(blocks, axis, split_axis=0, concat_axis=0, tiled=True)
    return arrived.astype(jnp.float32).sum(axis=0)


def sum_at_owner(array, axis, dim):
    blocks = cut_along(array, dim, lax.axis_size(axis))
    arrived = lax.all_to_all(blocks, axis, split_axis=0, concat_axis=0, tiled=True)
    return arrived.sum(axis=0)


def silu_grad(value):
    sigma = jax.nn.sigmoid(value)
    return sigma * (1.0 + value * (1.0 - sigma))


def norm_rows(rows):
    wide = rows.astype(jnp.float32)
    factor = lax.rsqrt(jnp.mean(wide * wide, axis=-1, keepdims=True) + EPS)
    return (wide * factor, factor)


def norm_back(grad, normed, factor):
    return factor * (grad - normed * jnp.mean(grad * normed, axis=-1, keepdims=True))


def rounded(value):
    return lax.optimization_barrier(value.astype(jnp.bfloat16)).astype(jnp.float32)


def doc_counts(documents):
    length = documents.shape[0]
    places = jnp.arange(length, dtype=jnp.int32)
    change = jnp.concatenate([jnp.ones((1,), bool), documents[1:] != documents[:-1]])
    first = lax.cummax(jnp.where(change, places, 0), axis=0)
    return (places - first + 1).astype(jnp.float32)


def bucket_index(dest_owner, groups, capacity):
    onehot = (dest_owner[:, None] == jnp.arange(groups, dtype=jnp.int32)[None, :]).astype(jnp.int32)
    before = jnp.cumsum(onehot, axis=0) - onehot
    rank = jnp.sum(before * onehot, axis=1)
    return dest_owner * capacity + rank


def tile_mask(documents, q_start, k_start, q_len, k_len):
    q_docs = documents[q_start : q_start + q_len]
    k_docs = documents[k_start : k_start + k_len]
    q_place = q_start + jnp.arange(q_len, dtype=jnp.int32)
    k_place = k_start + jnp.arange(k_len, dtype=jnp.int32)
    return (q_docs[:, None] == k_docs[None, :]) & (k_place[None, :] <= q_place[:, None])


def tile_forward(query, keys, values, allowed):
    scores = jnp.einsum(
        "hqd,hkd->hqk", query, keys, preferred_element_type=jnp.float32
    ) * query.shape[-1] ** (-0.5)
    weights = jnp.where(allowed[None], jax.nn.silu(scores), 0.0).astype(jnp.bfloat16)
    return jnp.einsum("hqk,hkd->hqd", weights, values, preferred_element_type=jnp.float32)


def tile_backward(query, keys, values, d_attended, allowed):
    head_scale = query.shape[-1] ** (-0.5)
    scores = (
        jnp.einsum("hqd,hkd->hqk", query, keys, preferred_element_type=jnp.float32) * head_scale
    )
    weights = jnp.where(allowed[None], jax.nn.silu(scores), 0.0).astype(jnp.bfloat16)
    d_weights = jnp.einsum("hqd,hkd->hqk", d_attended, values, preferred_element_type=jnp.float32)
    d_scores = jnp.where(allowed[None], d_weights * silu_grad(scores), 0.0).astype(jnp.bfloat16)
    d_query = (
        jnp.einsum("hqk,hkd->hqd", d_scores, keys, preferred_element_type=jnp.float32) * head_scale
    )
    d_keys = (
        jnp.einsum("hqk,hqd->hkd", d_scores, query, preferred_element_type=jnp.float32) * head_scale
    )
    d_values = jnp.einsum("hqk,hqd->hkd", weights, d_attended, preferred_element_type=jnp.float32)
    return (d_query, d_keys, d_values)


def attend(query, keys, values, documents):
    length = query.shape[1]
    block = min(BLOCK, length)
    outputs = []
    for q_index in range(length // block):
        q_start = q_index * block
        query_block = query[:, q_start : q_start + block]
        limit = q_start + block
        allowed = tile_mask(documents, q_start, 0, block, limit)
        outputs.append(tile_forward(query_block, keys[:, :limit], values[:, :limit], allowed))
    return jnp.concatenate(outputs, axis=1)


def attend_back(query, keys, values, d_attended, documents):
    length = query.shape[1]
    block = min(BLOCK, length)
    d_query_parts = []
    d_keys = jnp.zeros(keys.shape, jnp.float32)
    d_values = jnp.zeros(values.shape, jnp.float32)
    for q_index in range(length // block):
        q_start = q_index * block
        query_block = query[:, q_start : q_start + block]
        d_att_block = d_attended[:, q_start : q_start + block]
        limit = q_start + block
        allowed = tile_mask(documents, q_start, 0, block, limit)
        part_q, part_k, part_v = tile_backward(
            query_block, keys[:, :limit], values[:, :limit], d_att_block, allowed
        )
        d_query_parts.append(part_q)
        d_keys = d_keys.at[:, :limit].add(part_k)
        d_values = d_values.at[:, :limit].add(part_v)
    return (jnp.concatenate(d_query_parts, axis=1), d_keys, d_values)


def shards(
    features,
    dest_owner,
    dest_slot,
    doc_ids,
    enc_weight,
    attn_in,
    attn_out,
    ffn_in,
    ffn_out,
    out_grad,
):
    layers = enc_weight.shape[0]
    activations = [features]
    layer = 0
    preact = jnp.dot(activations[-1], enc_weight[layer], preferred_element_type=jnp.float32)
    pre_acts = [preact]
    activations.append(jax.nn.silu(preact).astype(jnp.bfloat16))
    encoded = jnp.dot(
        activations[-1], enc_weight[layers - 1], preferred_element_type=jnp.float32
    ).astype(jnp.bfloat16)
    rows_dev, width = features.shape
    groups = lax.axis_size(("event", "pack"))
    mean_load = rows_dev // groups
    capacity = mean_load + mean_load // 2
    place = bucket_index(dest_owner, groups, capacity)
    send_rows = (
        jnp.zeros((groups * capacity, width), jnp.bfloat16)
        .at[place]
        .set(encoded)
        .reshape(groups, capacity, width)
    )
    send_slots = (
        jnp.full((groups * capacity,), rows_dev, jnp.int32)
        .at[place]
        .set(dest_slot)
        .reshape(groups, capacity)
    )
    got_rows, got_slots = (
        lax.all_to_all(send_rows, ("event", "pack"), split_axis=0, concat_axis=0, tiled=True),
        lax.all_to_all(send_slots, ("event", "pack"), split_axis=0, concat_axis=0, tiled=True),
    )
    got_rows = got_rows.reshape(groups * capacity, width)
    got_slots = got_slots.reshape(groups * capacity)
    quarter = jnp.zeros((rows_dev, width), jnp.bfloat16).at[got_slots].set(got_rows, mode="drop")
    documents = doc_ids[0]
    root = jnp.sqrt(doc_counts(documents))[:, None]
    normed_f, factor1 = norm_rows(quarter)
    normed = normed_f.astype(jnp.bfloat16)
    projected = jnp.einsum(
        "rd,kdc->krc",
        gather_directly(normed, "tensor", 0),
        attn_in,
        preferred_element_type=jnp.float32,
    ).astype(jnp.bfloat16)
    length = projected.shape[1]
    local_cols = projected.shape[2]
    head_dim = D // HEADS
    local_heads = local_cols // head_dim

    def split_heads(value):
        return value.reshape(length, local_heads, head_dim).transpose(1, 0, 2)

    def join_heads(value):
        return value.transpose(1, 0, 2).reshape(length, local_cols)

    query = split_heads(projected[0])
    keys = split_heads(projected[1])
    values = split_heads(projected[2])
    gate_raw = projected[3].astype(jnp.float32)
    attended = join_heads(attend(query, keys, values, documents)) / root
    gated = (attended * jax.nn.silu(gate_raw)).astype(jnp.bfloat16)
    attn_sum = sent_and_summed(
        rounded(jnp.dot(gated, attn_out, preferred_element_type=jnp.float32)).astype(jnp.bfloat16),
        "tensor",
        0,
    )
    resid = (quarter.astype(jnp.float32) + attn_sum).astype(jnp.bfloat16)
    normed2_f, factor2 = norm_rows(resid)
    normed2 = normed2_f.astype(jnp.bfloat16)
    gate_up = jnp.einsum(
        "rd,kdf->krf",
        gather_directly(normed2, "tensor", 0),
        ffn_in,
        preferred_element_type=jnp.float32,
    )
    gate = gate_up[0]
    upper = gate_up[1]
    hidden = (jax.nn.silu(gate) * upper).astype(jnp.bfloat16)
    ffn_sum = sent_and_summed(
        rounded(jnp.dot(hidden, ffn_out, preferred_element_type=jnp.float32)).astype(jnp.bfloat16),
        "tensor",
        0,
    )
    packed_out = (resid.astype(jnp.float32) + ffn_sum).astype(jnp.bfloat16)
    d_out = out_grad[0]
    d_hidden = lax.dot_general(
        gather_directly(d_out, "tensor", 0),
        ffn_out,
        (((1,), (1,)), ((), ())),
        preferred_element_type=jnp.float32,
    )
    d_gate = (d_hidden * upper * silu_grad(gate)).astype(jnp.bfloat16)
    d_upper = (d_hidden * jax.nn.silu(gate)).astype(jnp.bfloat16)
    d_both = jnp.stack([d_gate, d_upper])
    piece = d_both
    d_normed2 = sent_and_summed(
        rounded(
            jnp.einsum("krf,kdf->rd", piece, ffn_in, preferred_element_type=jnp.float32)
        ).astype(jnp.bfloat16),
        "tensor",
        0,
    )
    d_resid = (d_out.astype(jnp.float32) + norm_back(d_normed2, normed2_f, factor2)).astype(
        jnp.bfloat16
    )
    d_gated = lax.dot_general(
        gather_directly(d_resid, "tensor", 0),
        attn_out,
        (((1,), (1,)), ((), ())),
        preferred_element_type=jnp.float32,
    )
    d_attended = (d_gated * jax.nn.silu(gate_raw) / root).astype(jnp.bfloat16)
    d_gate_proj = (d_gated * attended * silu_grad(gate_raw)).astype(jnp.bfloat16)
    d_query, d_keys, d_values = attend_back(query, keys, values, split_heads(d_attended), documents)
    d_projected = jnp.stack(
        [
            join_heads(d_query).astype(jnp.bfloat16),
            join_heads(d_keys).astype(jnp.bfloat16),
            join_heads(d_values).astype(jnp.bfloat16),
            d_gate_proj,
        ]
    )
    piece = d_projected
    d_normed = sent_and_summed(
        rounded(
            jnp.einsum("krc,kdc->rd", piece, attn_in, preferred_element_type=jnp.float32)
        ).astype(jnp.bfloat16),
        "tensor",
        0,
    )
    d_quarter = (d_resid.astype(jnp.float32) + norm_back(d_normed, normed_f, factor1)).astype(
        jnp.bfloat16
    )
    padded = jnp.concatenate([d_quarter, jnp.zeros((1, width), jnp.bfloat16)], axis=0)
    back_rows = padded[got_slots].reshape(groups, capacity, width)
    returned = lax.all_to_all(back_rows, ("event", "pack"), split_axis=0, concat_axis=0, tiled=True)
    row_grad = returned.reshape(groups * capacity, width)[place]
    tensor_count = lax.axis_size("tensor")
    cotangent = row_grad
    grads = []
    for layer in reversed(range(layers)):
        activation = activations[layer]

        def column_term(start, count, activation=activation, cotangent=cotangent):
            return lax.dot_general(
                cotangent, activation, (((0,), (0,)), ((), ())), preferred_element_type=jnp.float32
            )

        partial_cols = lax.psum_scatter(
            column_term(jnp.int32(0), width // tensor_count * lax.axis_size("tensor")).astype(
                jnp.bfloat16
            ),
            "tensor",
            scatter_dimension=0,
            tiled=True,
        ).astype(jnp.float32)
        grads.append(sum_at_owner(partial_cols, ("event", "pack"), 1).T)
        if layer > 0:
            back = lax.dot_general(
                cotangent,
                enc_weight[layer],
                (((1,), (1,)), ((), ())),
                preferred_element_type=jnp.float32,
            )
            cotangent = (back * silu_grad(pre_acts[layer - 1])).astype(jnp.bfloat16)
    enc_grad = jnp.stack(grads[::-1])
    return (packed_out[None], row_grad, enc_grad)


def solution(mesh):
    placed = (
        P(("event", "pack", "tensor"), None),
        P(("event", "pack", "tensor")),
        P(("event", "pack", "tensor")),
        P(("event", "pack"), None),
        P(),
        P(None, None, "tensor"),
        P("tensor", None),
        P(None, None, "tensor"),
        P("tensor", None),
        P(("event", "pack"), "tensor", None),
    )
    return jax.shard_map(
        shards,
        mesh=mesh,
        in_specs=placed,
        out_specs=(
            P(("event", "pack"), "tensor", None),
            P(("event", "pack", "tensor"), None),
            P(None, ("event", "pack"), "tensor"),
        ),
        check_vma=False,
    )
```

profile of v0, /device:TPU:8, one launch (start us, length us, event | category | flops | bytes accessed | tf_op | source)
XLA Modules:
  0.0 364.5 jit_solution(10349764470491832668)
XLA Ops:
  11.6 11.9 %all-to-all-start = ((s32[64,1,3]{2,1,0:T(1,128)}), s32[64,1,3]{2,1,0:T(1,128)S(1)}, u32[]{:S(2)}, u32[]{:S(2)}) async-start(s32[64,1,3]{2,1,0:T(1,128)} %bitcast), calls=%async_computation | async-start | bytes 65536 | tf_op jit(solution)/shard_map/all_to_all | solution.py:189
  23.6 2.1 fusion.4
  26.5 2.1 fusion.18
  28.6 1.3 scatter_custom_fusion.1
  30.9 2.2 all-to-all-done
  33.1 8.1 %all-to-all-start.1 = ((bf16[64,3,1024]{2,1,0:T(4,128)(2,1)}), bf16[64,3,1024]{2,1,0:T(4,128)(2,1)S(1)}, u32[]{:S(2)}, u32[]{:S(2)}) async-start(bf16[64,3,1024]{2,1,0:T(4,128)(2,1)} %reshape.439), calls=%async_computation.1 | async-start | bytes 1048576 | tf_op jit(solution)/shard_map/all_to_all | solution.py:188
  43.9 15.4 %all-to-all-done.1 = bf16[64,3,1024]{2,1,0:T(4,128)(2,1)S(1)} async-done(((bf16[64,3,1024]{2,1,0:T(4,128)(2,1)}), bf16[64,3,1024]{2,1,0:T(4,128)(2,1)S(1)}, u32[]{:S(2)}, u32[]{:S(2)}) %all-to-all-start.1) | async-done | bytes 393248 | tf_op jit(solution)/shard_map/all_to_all | solution.py:188
  59.6 1.5 scatter_custom_fusion.2
  62.4 4.9 %all-to-all-start.2 = ((bf16[4,128,1024]{2,1,0:T(8,128)(2,1)}), bf16[4,128,1024]{2,1,0:T(8,128)(2,1)S(1)}, u32[]{:S(2)}, u32[]{:S(2)}) async-start(bf16[4,128,1024]{2,1,0:T(8,128)(2,1)} %broadcast_in_dim.104), calls=%async_computation.2 | async-start | bytes 2097152 | tf_op jit(solution)/shard_map/all_to_all | solution.py:22
  68.3 11.9 %all-to-all-done.2 = bf16[4,128,1024]{2,1,0:T(8,128)(2,1)S(1)} async-done(((bf16[4,128,1024]{2,1,0:T(8,128)(2,1)}), bf16[4,128,1024]{2,1,0:T(8,128)(2,1)S(1)}, u32[]{:S(2)}, u32[]{:S(2)}) %all-to-all-start.2) | async-done | bytes 1048608 | tf_op jit(solution)/shard_map/all_to_all | solution.py:22
  80.2 2.9 fusion.9
  83.2 1.6 select_convert_fusion.2
  84.8 2.2 select_convert_fusion.1
  88.9 15.9 %all_to_all.69 = bf16[4,128,1024]{2,1,0:T(8,128)(2,1)S(1)} all-to-all(bf16[4,128,1024]{2,1,0:T(8,128)(2,1)S(1)} %bitcast.183), channel_id=1, replica_groups=mesh['event'=8,'pack'=8,'tensor'=4] {'tensor'}, dimensions={0} | all-to-all | bytes 2097152 | tf_op jit(solution)/shard_map/all_to_all | solution.py:37
  106.1 15.8 %all_to_all.70 = bf16[4,128,1024]{2,1,0:T(8,128)(2,1)} all-to-all(bf16[4,128,1024]{2,1,0:T(8,128)(2,1)S(1)} %broadcast_in_dim.109), channel_id=1, replica_groups=mesh['event'=8,'pack'=8,'tensor'=4] {'tensor'}, dimensions={0} | all-to-all | bytes 2097152 | tf_op jit(solution)/shard_map/all_to_all | solution.py:22
  121.8 1.2 broadcast_in_dim.111
  123.0 4.9 %all-to-all-start.6 = ((bf16[4,128,1024]{2,1,0:T(8,128)(2,1)}), bf16[4,128,1024]{2,1,0:T(8,128)(2,1)S(1)}, u32[]{:S(2)}, u32[]{:S(2)}) async-start(bf16[4,128,1024]{2,1,0:T(8,128)(2,1)} %broadcast_in_dim.111), calls=%async_computation.6 | async-start | bytes 2097152 | tf_op jit(solution)/shard_map/all_to_all | solution.py:22
  128.0 3.8 %convolution_bitcast_fusion = f32[2,512,512]{2,1,0:T(8,128)} fusion(bf16[512,1024,1]{1,0,2:T(8,128)(2,1)} %bitcast.181, bf16[2,1024,512]{2,1,0:T(8,128)(2,1)S(1)} %copy-done), kind=kOutput, calls=%fused_computation.25 | convolution fusion | flops 1073741824 | bytes 5242880 | tf_op jit(solution)/shard_map/rd,kdf->krf/dot_general | solution.py:229
  131.7 6.2 %all-to-all-done.6 = bf16[4,128,1024]{2,1,0:T(8,128)(2,1)S(1)} async-done(((bf16[4,128,1024]{2,1,0:T(8,128)(2,1)}), bf16[4,128,1024]{2,1,0:T(8,128)(2,1)S(1)}, u32[]{:S(2)}, u32[]{:S(2)}) %all-to-all-start.6) | async-done | bytes 1048608 | tf_op jit(solution)/shard_map/all_to_all | solution.py:22
  138.0 2.9 fusion.72
  140.9 2.3 bitcast_convert_fusion.1
  143.2 4.9 %all-to-all-start.7 = ((bf16[4,128,1024]{2,1,0:T(8,128)(2,1)}), bf16[4,128,1024]{2,1,0:T(8,128)(2,1)S(1)}, u32[]{:S(2)}, u32[]{:S(2)}) async-start(bf16[4,128,1024]{2,1,0:T(8,128)(2,1)} %bitcast.180), calls=%async_computation.7 | async-start | bytes 2097152 | tf_op jit(solution)/shard_map/all_to_all | solution.py:37
  148.2 3.6 convolution_convert_fusion.4
  151.8 5.8 %all-to-all-done.7 = bf16[4,128,1024]{2,1,0:T(8,128)(2,1)S(1)} async-done(((bf16[4,128,1024]{2,1,0:T(8,128)(2,1)}), bf16[4,128,1024]{2,1,0:T(8,128)(2,1)S(1)}, u32[]{:S(2)}, u32[]{:S(2)}) %all-to-all-start.7) | async-done | bytes 1048608 | tf_op jit(solution)/shard_map/all_to_all | solution.py:37
  158.6 5.7 %all-to-all-start.5 = ((bf16[4,128,1024]{2,1,0:T(8,128)(2,1)}), bf16[4,128,1024]{2,1,0:T(8,128)(2,1)}, u32[]{:S(2)}, u32[]{:S(2)}) async-start(bf16[4,128,1024]{2,1,0:T(8,128)(2,1)} %bitcast.177), calls=%async_computation.5 | async-start | bytes 2097152 | tf_op jit(solution)/shard_map/all_to_all | solution.py:37
  164.3 1.5 convert_reduce_fusion.1
  165.8 1.2 fusion.45
  166.9 6.9 %all-to-all-done.5 = bf16[4,128,1024]{2,1,0:T(8,128)(2,1)} async-done(((bf16[4,128,1024]{2,1,0:T(8,128)(2,1)}), bf16[4,128,1024]{2,1,0:T(8,128)(2,1)}, u32[]{:S(2)}, u32[]{:S(2)}) %all-to-all-start.5) | async-done | bytes 1048608 | tf_op jit(solution)/shard_map/all_to_all | solution.py:37
  173.8 1.5 convert_reduce_fusion.2
  176.4 13.4 %all_to_all.71 = bf16[4,128,1024]{2,1,0:T(8,128)(2,1)S(1)} all-to-all(bf16[4,128,1024]{2,1,0:T(8,128)(2,1)S(1)} %broadcast_in_dim.112), channel_id=1, replica_groups=mesh['event'=8,'pack'=8,'tensor'=4] {'tensor'}, dimensions={0} | all-to-all | bytes 2097152 | tf_op jit(solution)/shard_map/all_to_all | solution.py:22
  189.8 1.7 divide_convert_fusion
  193.6 1.1 select_convert_fusion
  196.7 2.3 bitcast_convert_fusion
  199.0 5.1 %all-to-all-start.9 = ((bf16[4,128,1024]{2,1,0:T(8,128)(2,1)}), bf16[4,128,1024]{2,1,0:T(8,128)(2,1)S(1)}, u32[]{:S(2)}, u32[]{:S(2)}) async-start(bf16[4,128,1024]{2,1,0:T(8,128)(2,1)} %bitcast.179), calls=%async_computation.9 | async-start | bytes 2097152 | tf_op jit(solution)/shard_map/all_to_all | solution.py:37
  204.1 9.4 %all-to-all-done.9 = bf16[4,128,1024]{2,1,0:T(8,128)(2,1)S(1)} async-done(((bf16[4,128,1024]{2,1,0:T(8,128)(2,1)}), bf16[4,128,1024]{2,1,0:T(8,128)(2,1)S(1)}, u32[]{:S(2)}, u32[]{:S(2)}) %all-to-all-start.9) | async-done | bytes 1048608 | tf_op jit(solution)/shard_map/all_to_all | solution.py:37
  216.8 13.4 %all-to-all-start.10 = ((bf16[64,3,1024]{2,1,0:T(4,128)(2,1)}), bf16[64,3,1024]{2,1,0:T(4,128)(2,1)S(1)}, u32[]{:S(2)}, u32[]{:S(2)}) async-start(bf16[64,3,1024]{2,1,0:T(4,128)(2,1)} %reshape.452), calls=%async_computation.10 | async-start | bytes 1048576 | tf_op jit(solution)/shard_map/all_to_all | solution.py:295
  230.5 17.8 %all-to-all-done.10 = bf16[64,3,1024]{2,1,0:T(4,128)(2,1)S(1)} async-done(((bf16[64,3,1024]{2,1,0:T(4,128)(2,1)}), bf16[64,3,1024]{2,1,0:T(4,128)(2,1)S(1)}, u32[]{:S(2)}, u32[]{:S(2)}) %all-to-all-start.10) | async-done | bytes 393248 | tf_op jit(solution)/shard_map/all_to_all | solution.py:295
  249.5 3.3 convolution_convert_fusion
  252.9 4.3 %convolution_convert_fusion.1 = bf16[1024,1024]{1,0:T(8,128)(2,1)} fusion(bf16[128,1024]{1,0:T(8,128)(2,1)S(1)} %copy-done.31, bf16[128,1024]{1,0:T(8,128)(2,1)S(1)} %gather_fusion.1, bf16[2,1024,1024]{2,1,0:T(8,128)(2,1)} %param.26, f32[128,1024]{1,0:T(8,128)S(1)} %copy-done.33), kind=kOutput, calls=%fused_computation.22 | convolution fusion | flops 539099136 | bytes 5242880 | tf_op jit(solution)/shard_map/dot_general | solution.py:304
  257.3 22.3 %reduce-scatter.5.cloned.1.call-done = bf16[256,1024]{1,0:T(8,128)(2,1)} async-done(((bf16[1024,1024]{1,0:T(8,128)(2,1)}), bf16[256,1024]{1,0:T(8,128)(2,1)}) %reduce-scatter.5.cloned.1.call-update) | async-done | bytes 524304 | tf_op jit(solution)/shard_map/reduce_scatter | solution.py:308
  279.5 2.2 copy.23
  281.8 10.4 %all-to-all-start.12 = ((f32[64,256,16]{1,2,0:T(8,128)}), f32[64,256,16]{1,2,0:T(8,128)S(1)}, u32[]{:S(2)}, u32[]{:S(2)}) async-start(f32[64,256,16]{1,2,0:T(8,128)} %bitcast.167), calls=%async_computation.14 | async-start | bytes 2097152 | tf_op jit(solution)/shard_map/all_to_all | solution.py:43
  292.2 21.9 %reduce-scatter.3.cloned.1.call-done = bf16[256,1024]{1,0:T(8,128)(2,1)} async-done(((bf16[1024,1024]{1,0:T(8,128)(2,1)}), bf16[256,1024]{1,0:T(8,128)(2,1)}) %reduce-scatter.3.cloned.1.call-update) | async-done | bytes 524304 | tf_op jit(solution)/shard_map/reduce_scatter | solution.py:308
  314.1 2.3 copy.22
  316.4 4.3 %all-to-all-done.12 = f32[64,256,16]{1,2,0:T(8,128)S(1)} async-done(((f32[64,256,16]{1,2,0:T(8,128)}), f32[64,256,16]{1,2,0:T(8,128)S(1)}, u32[]{:S(2)}, u32[]{:S(2)}) %all-to-all-start.12) | async-done | bytes 1048608 | tf_op jit(solution)/shard_map/all_to_all | solution.py:43
  320.7 6.7 %all-to-all-start.11 = ((f32[64,256,16]{1,2,0:T(8,128)}), f32[64,256,16]{1,2,0:T(8,128)}, u32[]{:S(2)}, u32[]{:S(2)}) async-start(f32[64,256,16]{1,2,0:T(8,128)} %bitcast.166), calls=%async_computation.12 | async-start | bytes 2097152 | tf_op jit(solution)/shard_map/all_to_all | solution.py:43
  327.5 28.2 %all-to-all-done.11 = f32[64,256,16]{1,2,0:T(8,128)} async-done(((f32[64,256,16]{1,2,0:T(8,128)}), f32[64,256,16]{1,2,0:T(8,128)}, u32[]{:S(2)}, u32[]{:S(2)}) %all-to-all-start.11) | async-done | bytes 1048608 | tf_op jit(solution)/shard_map/all_to_all | solution.py:43
  355.7 1.3 reduce_sum.108
  (138 shorter events, 26.3 us)
Async XLA Ops:
  7.2 120.8 %copy-start = (bf16[2,1024,512]{2,1,0:T(8,128)(2,1)S(1)}, bf16[2,1024,512]{2,1,0:T(8,128)(2,1)}, u32[]{:S(2)}) copy-start(bf16[2,1024,512]{2,1,0:T(8,128)(2,1)} %param.29) | copy-start | bytes 6291460
  9.7 18.8 %copy-start.26 = (s32[128]{0:T(128)}, s32[128]{0:T(128)S(1)}, u32[]{:S(2)}) copy-start(s32[128]{0:T(128)S(1)} %compare_select_fusion.2) | copy-start | bytes 1540
  11.6 21.5 %all-to-all-start = ((s32[64,1,3]{2,1,0:T(1,128)}), s32[64,1,3]{2,1,0:T(1,128)S(1)}, u32[]{:S(2)}, u32[]{:S(2)}) async-start(s32[64,1,3]{2,1,0:T(1,128)} %bitcast), calls=%async_computation | async-start | bytes 65536 | tf_op jit(solution)/shard_map/all_to_all | solution.py:189
  25.7 0.8 copy-start.32
  28.6 12.6 %copy-start.24 = (s32[1,512]{1,0:T(1,128)S(1)}, s32[1,512]{1,0:T(1,128)}, u32[]{:S(2)}) copy-start(s32[1,512]{1,0:T(1,128)} %param.25) | copy-start | bytes 6148
  33.1 26.2 %all-to-all-start.1 = ((bf16[64,3,1024]{2,1,0:T(4,128)(2,1)}), bf16[64,3,1024]{2,1,0:T(4,128)(2,1)S(1)}, u32[]{:S(2)}, u32[]{:S(2)}) async-start(bf16[64,3,1024]{2,1,0:T(4,128)(2,1)} %reshape.439), calls=%async_computation.1 | async-start | bytes 1048576 | tf_op jit(solution)/shard_map/all_to_all | solution.py:188
  62.4 17.8 %all-to-all-start.2 = ((bf16[4,128,1024]{2,1,0:T(8,128)(2,1)}), bf16[4,128,1024]{2,1,0:T(8,128)(2,1)S(1)}, u32[]{:S(2)}, u32[]{:S(2)}) async-start(bf16[4,128,1024]{2,1,0:T(8,128)(2,1)} %broadcast_in_dim.104), calls=%async_computation.2 | async-start | bytes 2097152 | tf_op jit(solution)/shard_map/all_to_all | solution.py:22
  80.2 3.0 copy-start.22
  83.1 4.7 %copy-start.18 = (bf16[4,512,256]{1,2,0:T(8,128)(2,1)}, bf16[4,512,256]{1,2,0:T(8,128)(2,1)S(1)}, u32[]{:S(2)}) copy-start(bf16[4,512,256]{1,2,0:T(8,128)(2,1)S(1)} %fusion.9) | copy-start | bytes 3145732
  83.2 1.6 copy-start.12
  83.2 1.6 copy-start.16
  83.2 4.0 %copy-start.10 = (bf16[1,512,256]{1,2,0:T(8,128)(2,1)}, bf16[1,512,256]{1,2,0:T(8,128)(2,1)S(1)}, u32[]{:S(2)}) copy-start(bf16[1,512,256]{1,2,0:T(8,128)(2,1)S(1)} %get-tuple-element.73) | copy-start | bytes 786436
  84.8 2.2 copy-start.8
  87.0 1.0 copy-start.1
  87.0 1.4 copy-start.29
  88.4 16.4 %copy-start.19 = (f32[512,256]{0,1:T(8,128)}, f32[512,256]{0,1:T(8,128)S(1)}, u32[]{:S(2)}) copy-start(f32[512,256]{0,1:T(8,128)S(1)} %bitcast_divide_fusion) | copy-start | bytes 1572868
  105.1 0.7 copy-start.4
  105.1 16.7 %copy-start.14 = (bf16[1,128,1024]{2,1,0:T(8,128)(2,1)S(1)}, bf16[1,128,1024]{2,1,0:T(8,128)(2,1)}, u32[]{:S(2)}) copy-start(bf16[1,128,1024]{2,1,0:T(8,128)(2,1)} %param.31) | copy-start | bytes 786436
  123.0 15.0 %all-to-all-start.6 = ((bf16[4,128,1024]{2,1,0:T(8,128)(2,1)}), bf16[4,128,1024]{2,1,0:T(8,128)(2,1)S(1)}, u32[]{:S(2)}, u32[]{:S(2)}) async-start(bf16[4,128,1024]{2,1,0:T(8,128)(2,1)} %broadcast_in_dim.111), calls=%async_computation.6 | async-start | bytes 2097152 | tf_op jit(solution)/shard_map/all_to_all | solution.py:22
  143.2 14.4 %all-to-all-start.7 = ((bf16[4,128,1024]{2,1,0:T(8,128)(2,1)}), bf16[4,128,1024]{2,1,0:T(8,128)(2,1)S(1)}, u32[]{:S(2)}, u32[]{:S(2)}) async-start(bf16[4,128,1024]{2,1,0:T(8,128)(2,1)} %bitcast.180), calls=%async_computation.7 | async-start | bytes 2097152 | tf_op jit(solution)/shard_map/all_to_all | solution.py:37
  157.6 1.0 copy-start.3
  158.6 15.2 %all-to-all-start.5 = ((bf16[4,128,1024]{2,1,0:T(8,128)(2,1)}), bf16[4,128,1024]{2,1,0:T(8,128)(2,1)}, u32[]{:S(2)}, u32[]{:S(2)}) async-start(bf16[4,128,1024]{2,1,0:T(8,128)(2,1)} %bitcast.177), calls=%async_computation.5 | async-start | bytes 2097152 | tf_op jit(solution)/shard_map/all_to_all | solution.py:37
  164.3 11.0 %copy-start.5 = (bf16[128,1024]{1,0:T(8,128)(2,1)S(1)}, bf16[128,1024]{1,0:T(8,128)(2,1)}, u32[]{:S(2)}) copy-start(bf16[128,1024]{1,0:T(8,128)(2,1)} %copy-done.4) | copy-start | bytes 786436
  164.3 11.0 %copy-start.15 = (bf16[1,128,1024]{2,1,0:T(8,128)(2,1)S(1)}, bf16[1,128,1024]{2,1,0:T(8,128)(2,1)}, u32[]{:S(2)}) copy-start(bf16[1,128,1024]{2,1,0:T(8,128)(2,1)} %param.31) | copy-start | bytes 786436
  176.2 15.3 %copy-start.6 = (bf16[128,1024]{1,0:T(8,128)(2,1)}, bf16[128,1024]{1,0:T(8,128)(2,1)S(1)}, u32[]{:S(2)}) copy-start(bf16[128,1024]{1,0:T(8,128)(2,1)S(1)} %get-tuple-element.76) | copy-start | bytes 786436
  176.2 13.6 %copy-start.20 = (f32[512,256]{0,1:T(8,128)S(1)}, f32[512,256]{0,1:T(8,128)}, u32[]{:S(2)}) copy-start(f32[512,256]{0,1:T(8,128)} %copy-done.19) | copy-start | bytes 1572868
  176.2 13.6 %copy-start.30 = (bf16[256,1024]{1,0:T(8,128)(2,1)S(1)}, bf16[256,1024]{1,0:T(8,128)(2,1)}, u32[]{:S(2)}) copy-start(bf16[256,1024]{1,0:T(8,128)(2,1)} %param.28) | copy-start | bytes 1572868
  189.8 1.8 copy-start.9
  189.8 2.0 copy-start.11
  189.8 2.0 copy-start.23
  189.8 2.0 copy-start.34
  191.8 1.0 copy-start.13
  191.8 1.2 copy-start.17
  191.8 1.8 copy-start.35
  193.6 1.2 copy-start.2
  195.1 1.6 copy-start.28
  199.0 5.1 %copy-start.25 = (s32[192,1]{0,1:T(1,128)S(1)}, s32[192,1]{0,1:T(1,128)}, u32[]{:S(2)}) copy-start(s32[192,1]{0,1:T(1,128)} %get-tuple-element.80) | copy-start | bytes 2308
  199.0 14.5 %all-to-all-start.9 = ((bf16[4,128,1024]{2,1,0:T(8,128)(2,1)}), bf16[4,128,1024]{2,1,0:T(8,128)(2,1)S(1)}, u32[]{:S(2)}, u32[]{:S(2)}) async-start(bf16[4,128,1024]{2,1,0:T(8,128)(2,1)} %bitcast.179), calls=%async_computation.9 | async-start | bytes 2097152 | tf_op jit(solution)/shard_map/all_to_all | solution.py:37
  213.5 1.0 copy-start.7
  214.7 15.8 %copy-start.27 = (s32[128]{0:T(128)S(1)}, s32[128]{0:T(128)}, u32[]{:S(2)}) copy-start(s32[128]{0:T(128)} %copy-done.26) | copy-start | bytes 1540
  216.8 31.5 %all-to-all-start.10 = ((bf16[64,3,1024]{2,1,0:T(4,128)(2,1)}), bf16[64,3,1024]{2,1,0:T(4,128)(2,1)S(1)}, u32[]{:S(2)}, u32[]{:S(2)}) async-start(bf16[64,3,1024]{2,1,0:T(4,128)(2,1)} %reshape.452), calls=%async_computation.10 | async-start | bytes 1048576 | tf_op jit(solution)/shard_map/all_to_all | solution.py:295
  230.3 49.3 %reduce-scatter.5.cloned.1.call-start = ((), (), s32[]{:S(2)}) async-start(), calls=%async_computation.16 | async-start | bytes 2621440 | tf_op jit(solution)/shard_map/reduce_scatter | solution.py:308
  249.5 3.4 copy-start.21
  249.5 3.4 copy-start.31
  249.5 3.4 copy-start.33
  252.8 61.3 %reduce-scatter.3.cloned.1.call-start = ((), (), s32[]{:S(2)}) async-start(), calls=%async_computation.15 | async-start | bytes 2621440 | tf_op jit(solution)/shard_map/reduce_scatter | solution.py:308
  281.8 38.9 %all-to-all-start.12 = ((f32[64,256,16]{1,2,0:T(8,128)}), f32[64,256,16]{1,2,0:T(8,128)S(1)}, u32[]{:S(2)}, u32[]{:S(2)}) async-start(f32[64,256,16]{1,2,0:T(8,128)} %bitcast.167), calls=%async_computation.14 | async-start | bytes 2097152 | tf_op jit(solution)/shard_map/all_to_all | solution.py:43
  320.7 35.0 %all-to-all-start.11 = ((f32[64,256,16]{1,2,0:T(8,128)}), f32[64,256,16]{1,2,0:T(8,128)}, u32[]{:S(2)}, u32[]{:S(2)}) async-start(f32[64,256,16]{1,2,0:T(8,128)} %bitcast.166), calls=%async_computation.12 | async-start | bytes 2097152 | tf_op jit(solution)/shard_map/all_to_all | solution.py:43
Sparse Core Ops, SparseCore 0:
  252.9 26.5 reduce-scatter.4
  282.1 31.9 reduce-scatter.2
where the time goes:
time: 368 us; the launch traced here: 364 us
  waiting for transfers between devices  152 us (41%)
  starting transfers between devices  76.4 us (21%)
  blocking collectives  45.1 us (12%)
  matrix products  39.7 us (11%)
  local copies, waits for them, and re-layouts  22.3 us (6%)
  between operations  14.7 us (4%)
  other arithmetic  14 us (4%)
    reduce_scatter x2, waiting for transfers between devices, shards(): lax.psum_scatter(column_term(jnp.int32(0), width // tensor_count * lax.ax...  44.2 us
    all_to_all x2, waiting for transfers between devices, sum_at_owner(): lax.all_to_all(blocks, axis, split_axis=0, concat_axis=0, tiled=True)  32.5 us
    all_to_all x2, blocking collectives, sent_to_all(): return lax.all_to_all(copies, axis, split_axis=0, concat_axis=0, tiled=True)  29.2 us
    all_to_all x3, waiting for transfers between devices, sent_and_summed(): lax.all_to_all(blocks, axis, split_axis=0, concat_axis=0, tiled=True)  22.1 us
    all_to_all x2, waiting for transfers between devices, sent_to_all(): return lax.all_to_all(copies, axis, split_axis=0, concat_axis=0, tiled=True)  18.1 us
    all_to_all x1, waiting for transfers between devices, shards(): lax.all_to_all(back_rows, ('event', 'pack'), split_axis=0, concat_axis=0,...  17.8 us
    all_to_all x2, starting transfers between devices, sum_at_owner(): lax.all_to_all(blocks, axis, split_axis=0, concat_axis=0, tiled=True)  17.1 us
    all_to_all x1, blocking collectives, sent_and_summed(): lax.all_to_all(blocks, axis, split_axis=0, concat_axis=0, tiled=True)  15.9 us
  transfers between devices with their start and end apart: 12, of which 12 were waited for; matrix products, arithmetic and copies ran while one was open for 8% of the time, Pallas kernels for 0%

commit v1 on v0

--- a/solution.py
+++ b/solution.py
@@ -1,6 +1,8 @@
 import jax
 import jax.numpy as jnp
 from jax import lax
+from jax.experimental import pallas as pl
+from jax.experimental.pallas import tpu as pltpu
 from jax.sharding import PartitionSpec as P
 
 D = 1024
@@ -36,12 +38,6 @@
     blocks = cut_along(array, dim, lax.axis_size(axis))
     arrived = lax.all_to_all(blocks, axis, split_axis=0, concat_axis=0, tiled=True)
     return arrived.astype(jnp.float32).sum(axis=0)
-
-
-def sum_at_owner(array, axis, dim):
-    blocks = cut_along(array, dim, lax.axis_size(axis))
-    arrived = lax.all_to_all(blocks, axis, split_axis=0, concat_axis=0, tiled=True)
-    return arrived.sum(axis=0)
 
 
 def silu_grad(value):
@@ -69,13 +65,6 @@
     change = jnp.concatenate([jnp.ones((1,), bool), documents[1:] != documents[:-1]])
     first = lax.cummax(jnp.where(change, places, 0), axis=0)
     return (places - first + 1).astype(jnp.float32)
-
-
-def bucket_index(dest_owner, groups, capacity):
-    onehot = (dest_owner[:, None] == jnp.arange(groups, dtype=jnp.int32)[None, :]).astype(jnp.int32)
-    before = jnp.cumsum(onehot, axis=0) - onehot
-    rank = jnp.sum(before * onehot, axis=1)
-    return dest_owner * capacity + rank
 
 
 def tile_mask(documents, q_start, k_start, q_len, k_len):
@@ -146,6 +135,474 @@
     return (jnp.concatenate(d_query_parts, axis=1), d_keys, d_values)
 
 
+MESH = pl.DeviceIdType.MESH
+GROUPS = 64
+CAP = 3
+BLOCK_ROWS = CAP * 8
+VMEM_LIMIT = 60 * 1024 * 1024
+
+
+def where_am_i():
+    return (lax.axis_index("event"), lax.axis_index("pack"), lax.axis_index("tensor"))
+
+
+def peer(index, tensor):
+    return (index // 8, lax.rem(index, 8), tensor)
+
+
+def greet_all(barrier, me, tensor):
+    def greet(step, carry):
+        pl.semaphore_signal(
+            barrier, inc=1, device_id=peer(lax.rem(me + step, GROUPS), tensor), device_id_type=MESH
+        )
+        return carry
+
+    lax.fori_loop(1, GROUPS, greet, 0)
+
+
+def exchange_copy(source, target, me, tensor, step, send_sem, recv_sem):
+    other = lax.rem(me + step, GROUPS)
+    return pltpu.make_async_remote_copy(
+        src_ref=source.at[other],
+        dst_ref=target.at[me],
+        send_sem=send_sem,
+        recv_sem=recv_sem,
+        device_id=peer(other, tensor),
+        device_id_type=MESH,
+    )
+
+
+def start_exchange(source, target, me, tensor, send_sem, recv_sem):
+    def start(step, carry):
+        exchange_copy(source, target, me, tensor, step, send_sem, recv_sem).start()
+        return carry
+
+    lax.fori_loop(1, GROUPS, start, 0)
+    target[me] = source[me]
+
+
+def await_bytes(ref, sem):
+    pltpu.make_async_copy(ref, ref, sem).wait()
+
+
+def end_exchange(source, target, send_sem, recv_sem):
+    await_bytes(source.at[pl.ds(0, GROUPS - 1)], send_sem)
+    await_bytes(target.at[pl.ds(0, GROUPS - 1)], recv_sem)
+
+
+def dot32(left, right, dims=((1,), (0,))):
+    return lax.dot_general(left, right, (dims, ((), ())), preferred_element_type=jnp.float32)
+
+
+def routing(owner_row):
+    rows = jnp.broadcast_to(owner_row, (128, 128))
+    columns = rows.T
+    earlier = lax.broadcasted_iota(jnp.int32, (128, 128), 0) < lax.broadcasted_iota(
+        jnp.int32, (128, 128), 1
+    )
+    rank = jnp.sum(jnp.where((columns == rows) & earlier, 1.0, 0.0), axis=0, keepdims=True)
+    group = lax.broadcasted_iota(jnp.int32, (GROUPS, 128), 0).astype(jnp.float32)
+    mine = owner_row == group
+    return [mine & (rank == float(k)) for k in range(CAP)]
+
+
+def one_hot(mask):
+    return jnp.where(mask, 1.0, 0.0).astype(jnp.bfloat16)
+
+
+def spread_rows(wide, k, rows):
+    for part in range(8):
+        wide[pl.ds(k * 8 + part, GROUPS, stride=BLOCK_ROWS), :] = rows[
+            :, part * 128 : (part + 1) * 128
+        ]
+
+
+def joined_rows(wide, k):
+    return jnp.concatenate(
+        [wide[pl.ds(k * 8 + part, GROUPS, stride=BLOCK_ROWS), :] for part in range(8)], axis=1
+    ).astype(jnp.bfloat16)
+
+
+def silu(value):
+    return value * jax.nn.sigmoid(value)
+
+
+def dispatch_kernel(
+    features,
+    owner,
+    slot,
+    weight_hbm,
+    quarter,
+    preact,
+    activation,
+    got_slots,
+    weight,
+    wide,
+    send_rows,
+    got_rows,
+    send_slots,
+    load_sem,
+    send_sem,
+    recv_sem,
+):
+    event, pack, tensor = where_am_i()
+    me = event * 8 + pack
+    barrier = pltpu.get_barrier_semaphore()
+    loads = []
+    for layer in range(2):
+        load = pltpu.make_async_copy(weight_hbm.at[layer], weight.at[layer], load_sem.at[layer])
+        load.start()
+        loads.append(load)
+    greet_all(barrier, me, tensor)
+    picks = routing(owner[...].astype(jnp.float32))
+    slot_row = slot[...].astype(jnp.float32) + 1.0
+    lane = lax.broadcasted_iota(jnp.int32, (GROUPS, 128), 1)
+    slots = jnp.full((GROUPS, 128), -1.0, jnp.float32)
+    for k in range(CAP):
+        value = jnp.sum(jnp.where(picks[k], slot_row, 0.0), axis=1, keepdims=True) - 1.0
+        slots = jnp.where(lane == k, value, slots)
+    send_slots[:, 0, :] = slots
+    loads[0].wait()
+    pre = dot32(features[...], weight[0])
+    preact[...] = pre
+    act = silu(pre).astype(jnp.bfloat16)
+    activation[...] = act
+    loads[1].wait()
+    encoded = dot32(act, weight[1]).astype(jnp.bfloat16)
+    for k in range(CAP):
+        spread_rows(wide, k, dot32(one_hot(picks[k]), encoded))
+    send_rows[...] = wide[...].astype(jnp.bfloat16).reshape(GROUPS, BLOCK_ROWS, 128)
+    pl.semaphore_wait(barrier, GROUPS - 1)
+    start_exchange(send_slots, got_slots, me, tensor, send_sem.at[0], recv_sem.at[0])
+    start_exchange(send_rows, got_rows, me, tensor, send_sem.at[1], recv_sem.at[1])
+    end_exchange(send_slots, got_slots, send_sem.at[0], recv_sem.at[0])
+    end_exchange(send_rows, got_rows, send_sem.at[1], recv_sem.at[1])
+    wide[...] = got_rows[...].reshape(GROUPS * BLOCK_ROWS, 128).astype(jnp.float32)
+    turned = jnp.concatenate(
+        [got_slots[:, 0, :], jnp.full((GROUPS, 128), -1.0, jnp.float32)], axis=0
+    ).T
+    place = lax.broadcasted_iota(jnp.int32, (128, GROUPS), 0).astype(jnp.float32)
+    total = None
+    for k in range(CAP):
+        pick = one_hot(turned[k : k + 1, :GROUPS] == place)
+        term = dot32(pick, joined_rows(wide, k))
+        total = term if total is None else total + term
+    quarter[...] = total.astype(jnp.bfloat16)
+
+
+def dispatch(features, owner, slot, enc_weight):
+    vmem = pl.BlockSpec(memory_space=pltpu.VMEM)
+    return pl.pallas_call(
+        dispatch_kernel,
+        out_shape=(
+            jax.ShapeDtypeStruct((128, 1024), jnp.bfloat16),
+            jax.ShapeDtypeStruct((128, 1024), jnp.float32),
+            jax.ShapeDtypeStruct((128, 1024), jnp.bfloat16),
+            jax.ShapeDtypeStruct((GROUPS, 1, 128), jnp.float32),
+        ),
+        in_specs=[vmem, vmem, vmem, pl.BlockSpec(memory_space=pl.ANY)],
+        out_specs=(vmem, vmem, vmem, vmem),
+        scratch_shapes=[
+            pltpu.VMEM((2, 1024, 1024), jnp.bfloat16),
+            pltpu.VMEM((GROUPS * BLOCK_ROWS, 128), jnp.float32),
+            pltpu.VMEM((GROUPS, BLOCK_ROWS, 128), jnp.bfloat16),
+            pltpu.VMEM((GROUPS, BLOCK_ROWS, 128), jnp.bfloat16),
+            pltpu.VMEM((GROUPS, 1, 128), jnp.float32),
+            pltpu.SemaphoreType.DMA((2,)),
+            pltpu.SemaphoreType.DMA((2,)),
+            pltpu.SemaphoreType.DMA((2,)),
+        ],
+        compiler_params=pltpu.CompilerParams(
+            collective_id=0, has_side_effects=True, vmem_limit_bytes=VMEM_LIMIT
+        ),
+        name="dispatch",
+    )(features, owner.reshape(1, 128), slot.reshape(1, 128), enc_weight)
+
+
+class Halving:
+    def __init__(self, blocks, first, second, outgoing, sems, base, index, device):
+        self.blocks, self.first, self.second, self.outgoing = blocks, first, second, outgoing
+        self.sems, self.base, self.index = sems, base, index
+        near = index + 1 - 2 * lax.rem(index, 2)
+        self.other = (near, 3 - index)
+        self.far = lax.rem(index + 2, 4)
+        self.device = device
+
+    def copy(self, source, target, number, half_partner):
+        send, recv = self.sems
+        return pltpu.make_async_remote_copy(
+            src_ref=source,
+            dst_ref=target,
+            send_sem=send.at[self.base + number],
+            recv_sem=recv.at[self.base + number],
+            device_id=self.device(half_partner),
+            device_id_type=MESH,
+        )
+
+    def round_one(self):
+        copies = []
+        for half in range(2):
+            partner = self.other[half]
+            for slot, block in enumerate((partner, self.far)):
+                copies.append(
+                    self.copy(
+                        self.blocks.at[block, half],
+                        self.first.at[half, slot],
+                        half * 2 + slot,
+                        partner,
+                    )
+                )
+        return copies
+
+    def round_two(self):
+        return [
+            self.copy(self.outgoing.at[half], self.second.at[half], 4 + half, self.other[1 - half])
+            for half in range(2)
+        ]
+
+    def start_one(self):
+        for copy in self.round_one():
+            copy.start()
+
+    def start_two(self):
+        for copy in self.round_one():
+            copy.wait()
+        for half in range(2):
+            block = self.other[1 - half]
+            self.outgoing[half] = (
+                self.blocks[block, half].astype(jnp.float32)
+                + self.first[half, 1].astype(jnp.float32)
+            ).astype(jnp.bfloat16)
+        for copy in self.round_two():
+            copy.start()
+
+    def finish(self):
+        for copy in self.round_two():
+            copy.wait()
+        return [
+            (
+                self.blocks[self.index, half].astype(jnp.float32)
+                + self.first[half, 0].astype(jnp.float32)
+                + self.second[half].astype(jnp.float32)
+            ).astype(jnp.bfloat16)
+            for half in range(2)
+        ]
+
+
+def back_kernel(
+    d_quarter,
+    got_slots,
+    owner,
+    features,
+    activation,
+    preact,
+    weight_hbm,
+    row_grad,
+    enc_grad,
+    weight,
+    wide,
+    send_rows,
+    got_rows,
+    acts,
+    cots,
+    grads,
+    firsts,
+    seconds,
+    outs,
+    grads2,
+    firsts2,
+    seconds2,
+    outs2,
+    send_z,
+    got_z,
+    load_sem,
+    send_sem,
+    recv_sem,
+    pair_send,
+    pair_recv,
+    half_send,
+    half_recv,
+    z_send,
+    z_recv,
+):
+    event, pack, tensor = where_am_i()
+    me = event * 8 + pack
+    core = lax.rem(event, 2)
+    chip_x = event // 2
+    partner = (event + 1 - 2 * core, pack, tensor)
+    barrier = pltpu.get_barrier_semaphore()
+    load = pltpu.make_async_copy(weight_hbm.at[1], weight, load_sem.at[0])
+    load.start()
+    greet_all(barrier, me, tensor)
+    for shift in (1, 3):
+        pl.semaphore_signal(
+            barrier,
+            inc=1,
+            device_id=(event, pack, lax.rem(tensor + shift, 4)),
+            device_id_type=MESH,
+        )
+
+    def pair_copy(number, array):
+        return pltpu.make_async_remote_copy(
+            src_ref=array.at[0],
+            dst_ref=array.at[1],
+            send_sem=pair_send.at[number],
+            recv_sem=pair_recv.at[number],
+            device_id=partner,
+            device_id_type=MESH,
+        )
+
+    acts[0, 0] = features[...]
+    acts[1, 0] = activation[...]
+    lane = lax.broadcasted_iota(jnp.int32, (GROUPS, 128), 1).astype(jnp.float32)
+    for k in range(CAP):
+        pick = one_hot(got_slots[:, 0, k : k + 1] == lane)
+        spread_rows(wide, k, dot32(pick, d_quarter[...]))
+    send_rows[...] = wide[...].astype(jnp.bfloat16).reshape(GROUPS, BLOCK_ROWS, 128)
+    pl.semaphore_wait(barrier, GROUPS - 1 + 2)
+    start_exchange(send_rows, got_rows, me, tensor, send_sem.at[0], recv_sem.at[0])
+    act_copies = [pair_copy(layer, acts.at[layer]) for layer in range(2)]
+    for copy in act_copies:
+        copy.start()
+    picks = routing(owner[...].astype(jnp.float32))
+    load.wait()
+    for copy in act_copies:
+        copy.wait()
+    end_exchange(send_rows, got_rows, send_sem.at[0], recv_sem.at[0])
+    wide[...] = got_rows[...].reshape(GROUPS * BLOCK_ROWS, 128).astype(jnp.float32)
+    total = None
+    for k in range(CAP):
+        term = dot32(one_hot(picks[k]), joined_rows(wide, k), ((0,), (0,)))
+        total = term if total is None else total + term
+    cotangent = total.astype(jnp.bfloat16)
+    row_grad[...] = cotangent
+    cots[1, 0] = cotangent
+    cot_copies = [pair_copy(2 + layer, cots.at[layer]) for layer in range(2)]
+    cot_copies[1].start()
+    pre = preact[...]
+    sigma = jax.nn.sigmoid(pre)
+    back = dot32(cotangent, weight[...], ((1,), (1,)))
+    cots[0, 0] = (back * (sigma * (1.0 + pre * (1.0 - sigma)))).astype(jnp.bfloat16)
+    cot_copies[0].start()
+
+    def tensor_device(index):
+        return (event, pack, index)
+
+    def chip_device(index):
+        return (index * 2 + core, pack, tensor)
+
+    rings = ((chip_x, chip_device), (tensor, tensor_device))
+    stages = [[], []]
+    for layer in range(2):
+        for stage, refs in enumerate(
+            ((grads, firsts, seconds, outs), (grads2, firsts2, seconds2, outs2))
+        ):
+            index, device = rings[layer] if stage == 0 else rings[1 - layer]
+            stages[stage].append(
+                Halving(
+                    *(ref.at[layer] for ref in refs),
+                    (half_send, half_recv),
+                    (stage * 2 + layer) * 6,
+                    index,
+                    device,
+                )
+            )
+    for layer in (1, 0):
+        cot_copies[layer].wait()
+        cot = cots[layer].reshape(256, 1024)
+        for chip in range(4):
+            columns = pl.ds(pl.multiple_of((chip * 2 + core) * 128, 128), 128)
+            act = acts[layer, :, :, columns].reshape(256, 128)
+            term = dot32(act, cot, ((0,), (0,))).astype(jnp.bfloat16)
+            for block in range(4):
+                for half in range(2):
+                    piece = term[half * 64 : (half + 1) * 64, block * 256 : (block + 1) * 256]
+                    if layer == 1:
+                        grads[layer, block, half, chip] = piece
+                    else:
+                        grads[layer, chip, half, block] = piece
+        stages[0][layer].start_one()
+    for layer in (1, 0):
+        stages[0][layer].start_two()
+    for layer in (1, 0):
+        for half, value in enumerate(stages[0][layer].finish()):
+            for block in range(4):
+                grads2[layer, block, half] = value[block]
+        stages[1][layer].start_one()
+    for layer in (1, 0):
+        stages[1][layer].start_two()
+    for layer in (1, 0):
+        for half, value in enumerate(stages[1][layer].finish()):
+            for quarter in range(4):
+                send_z[half * 4 + quarter, layer] = value[quarter * 16 : (quarter + 1) * 16]
+    z_copies = []
+    for step in (1, 7, 2, 6, 3, 5, 4):
+        other = lax.rem(pack + step, 8)
+        z_copies.append(
+            pltpu.make_async_remote_copy(
+                src_ref=send_z.at[other],
+                dst_ref=got_z.at[pack],
+                send_sem=z_send.at[step],
+                recv_sem=z_recv.at[step],
+                device_id=(event, other, tensor),
+                device_id_type=MESH,
+            )
+        )
+        z_copies[-1].start()
+    got_z[pack] = send_z[pack]
+    for copy in z_copies:
+        copy.wait()
+    total = got_z[0].astype(jnp.float32)
+    for source in range(1, 8):
+        total = total + got_z[source].astype(jnp.float32)
+    enc_grad[...] = total
+
+
+def give_back(d_quarter, got_slots, owner, features, activation, preact, enc_weight):
+    vmem = pl.BlockSpec(memory_space=pltpu.VMEM)
+    bf16 = jnp.bfloat16
+    return pl.pallas_call(
+        back_kernel,
+        out_shape=(
+            jax.ShapeDtypeStruct((128, 1024), bf16),
+            jax.ShapeDtypeStruct((2, 16, 256), jnp.float32),
+        ),
+        in_specs=[vmem] * 6 + [pl.BlockSpec(memory_space=pl.ANY)],
+        out_specs=(vmem, vmem),
+        scratch_shapes=[
+            pltpu.VMEM((1024, 1024), bf16),
+            pltpu.VMEM((GROUPS * BLOCK_ROWS, 128), jnp.float32),
+            pltpu.VMEM((GROUPS, BLOCK_ROWS, 128), bf16),
+            pltpu.VMEM((GROUPS, BLOCK_ROWS, 128), bf16),
+            pltpu.VMEM((2, 2, 128, 1024), bf16),
+            pltpu.VMEM((2, 2, 128, 1024), bf16),
+            pltpu.VMEM((2, 4, 2, 4, 64, 256), bf16),
+            pltpu.VMEM((2, 2, 2, 4, 64, 256), bf16),
+            pltpu.VMEM((2, 2, 4, 64, 256), bf16),
+            pltpu.VMEM((2, 2, 4, 64, 256), bf16),
+            pltpu.VMEM((2, 4, 2, 64, 256), bf16),
+            pltpu.VMEM((2, 2, 2, 64, 256), bf16),
+            pltpu.VMEM((2, 2, 64, 256), bf16),
+            pltpu.VMEM((2, 2, 64, 256), bf16),
+            pltpu.VMEM((8, 2, 16, 256), bf16),
+            pltpu.VMEM((8, 2, 16, 256), bf16),
+            pltpu.SemaphoreType.DMA((1,)),
+            pltpu.SemaphoreType.DMA((1,)),
+            pltpu.SemaphoreType.DMA((1,)),
+            pltpu.SemaphoreType.DMA((4,)),
+            pltpu.SemaphoreType.DMA((4,)),
+            pltpu.SemaphoreType.DMA((24,)),
+            pltpu.SemaphoreType.DMA((24,)),
+            pltpu.SemaphoreType.DMA((8,)),
+            pltpu.SemaphoreType.DMA((8,)),
+        ],
+        compiler_params=pltpu.CompilerParams(
+            collective_id=1, has_side_effects=True, vmem_limit_bytes=VMEM_LIMIT
+        ),
+        name="give_back",
+    )(d_quarter, got_slots, owner.reshape(1, 128), features, activation, preact, enc_weight)
+
+
 def shards(
     features,
     dest_owner,
@@ -158,39 +615,7 @@
     ffn_out,
     out_grad,
 ):
-    layers = enc_weight.shape[0]
-    activations = [features]
-    layer = 0
-    preact = jnp.dot(activations[-1], enc_weight[layer], preferred_element_type=jnp.float32)
-    pre_acts = [preact]
-    activations.append(jax.nn.silu(preact).astype(jnp.bfloat16))
-    encoded = jnp.dot(
-        activations[-1], enc_weight[layers - 1], preferred_element_type=jnp.float32
-    ).astype(jnp.bfloat16)
-    rows_dev, width = features.shape
-    groups = lax.axis_size(("event", "pack"))
-    mean_load = rows_dev // groups
-    capacity = mean_load + mean_load // 2
-    place = bucket_index(dest_owner, groups, capacity)
-    send_rows = (
-        jnp.zeros((groups * capacity, width), jnp.bfloat16)
-        .at[place]
-        .set(encoded)
-        .reshape(groups, capacity, width)
-    )
-    send_slots = (
-        jnp.full((groups * capacity,), rows_dev, jnp.int32)
-        .at[place]
-        .set(dest_slot)
-        .reshape(groups, capacity)
-    )
-    got_rows, got_slots = (
-        lax.all_to_all(send_rows, ("event", "pack"), split_axis=0, concat_axis=0, tiled=True),
-        lax.all_to_all(send_slots, ("event", "pack"), split_axis=0, concat_axis=0, tiled=True),
-    )
-    got_rows = got_rows.reshape(groups * capacity, width)
-    got_slots = got_slots.reshape(groups * capacity)
-    quarter = jnp.zeros((rows_dev, width), jnp.bfloat16).at[got_slots].set(got_rows, mode="drop")
+    quarter, preact, activation, got_slots = dispatch(features, dest_owner, dest_slot, enc_weight)
     documents = doc_ids[0]
     root = jnp.sqrt(doc_counts(documents))[:, None]
     normed_f, factor1 = norm_rows(quarter)
@@ -290,39 +715,9 @@
     d_quarter = (d_resid.astype(jnp.float32) + norm_back(d_normed, normed_f, factor1)).astype(
         jnp.bfloat16
     )
-    padded = jnp.concatenate([d_quarter, jnp.zeros((1, width), jnp.bfloat16)], axis=0)
-    back_rows = padded[got_slots].reshape(groups, capacity, width)
-    returned = lax.all_to_all(back_rows, ("event", "pack"), split_axis=0, concat_axis=0, tiled=True)
-    row_grad = returned.reshape(groups * capacity, width)[place]
-    tensor_count = lax.axis_size("tensor")
-    cotangent = row_grad
-    grads = []
-    for layer in reversed(range(layers)):
-        activation = activations[layer]
-
-        def column_term(start, count, activation=activation, cotangent=cotangent):
-            return lax.dot_general(
-                cotangent, activation, (((0,), (0,)), ((), ())), preferred_element_type=jnp.float32
-            )
-
-        partial_cols = lax.psum_scatter(
-            column_term(jnp.int32(0), width // tensor_count * lax.axis_size("tensor")).astype(
-                jnp.bfloat16
-            ),
-            "tensor",
-            scatter_dimension=0,
-            tiled=True,
-        ).astype(jnp.float32)
-        grads.append(sum_at_owner(partial_cols, ("event", "pack"), 1).T)
-        if layer > 0:
-            back = lax.dot_general(
-                cotangent,
-                enc_weight[layer],
-                (((1,), (1,)), ((), ())),
-                preferred_element_type=jnp.float32,
-            )
-            cotangent = (back * silu_grad(pre_acts[layer - 1])).astype(jnp.bfloat16)
-    enc_grad = jnp.stack(grads[::-1])
+    row_grad, enc_grad = give_back(
+        d_quarter, got_slots, dest_owner, features, activation, preact, enc_weight
+    )
     return (packed_out[None], row_grad, enc_grad)
 
 

time: 368 us -> 241 us (0.65)
  waiting for transfers between devices: 152 us -> 31.3 us
  Pallas kernels: 0 us -> 80.7 us
  starting transfers between devices: 76.4 us -> 20.4 us
  blocking collectives: 45.1 us -> 58.9 us
  between operations: 14.7 us -> 1.07 us
  matrix products: 39.7 us -> 26.9 us
  local copies, waits for them, and re-layouts: 22.3 us -> 9.65 us
  other arithmetic: 14 us -> 10.1 us
    pallas_call x0 -> x2, Pallas kernels: none -> 80.7 us  [the longest x1 56.1 us: give_back(): pl.pallas_call(back_kernel, out_shape=(jax.ShapeDtypeStruct((128, 1024),...]
    all_to_all x5 -> x0, waiting for transfers between devices: 67.9 us -> none  [the longest x2 32.5 us: sum_at_owner(): lax.all_to_all(blocks, axis, split_axis=0, concat_axis=0, tiled=True)]
    all_to_all x5 -> x0, starting transfers between devices: 50.6 us -> none  [the longest x2 17.1 us: sum_at_owner(): lax.all_to_all(blocks, axis, split_axis=0, concat_axis=0, tiled=True)]
    reduce_scatter x2 -> x0, waiting for transfers between devices: 44.2 us -> none  [shards(): lax.psum_scatter(column_term(jnp.int32(0), width // tensor_count * lax.ax...]
    all_to_all x1 -> x2, blocking collectives: 15.9 us -> 29.5 us  [sent_and_summed(): lax.all_to_all(blocks, axis, split_axis=0, concat_axis=0, tiled=True)]
    dot_general x4 -> x0, matrix products: 11.8 us -> none  [the longest x2 7.61 us: column_term(): lax.dot_general(cotangent, activation, (((0,), (0,)), ((), ())), preferre...]
    all_to_all x3 -> x2, waiting for transfers between devices: 22.1 us -> 12.7 us  [sent_and_summed(): lax.all_to_all(blocks, axis, split_axis=0, concat_axis=0, tiled=True)]
    all_to_all x3 -> x2, starting transfers between devices: 15.7 us -> 10.6 us  [sent_and_summed(): lax.all_to_all(blocks, axis, split_axis=0, concat_axis=0, tiled=True)]
  transfers between devices with their start and end apart: 12 -> 4, of which waited for: 12 -> 4; matrix products, arithmetic and copies ran while one was open for 8% -> 5% of each run, Pallas kernels for 0% -> 0%
where the time goes in v1:
time: 241 us; the launch traced here: 239 us
  Pallas kernels  80.7 us (33%)
  blocking collectives  58.9 us (24%)
  waiting for transfers between devices  31.3 us (13%)
  matrix products  26.9 us (11%)
  starting transfers between devices  20.4 us (8%)
  other arithmetic  10.1 us (4%)
  local copies, waits for them, and re-layouts  9.65 us (4%)
    pallas_call x1, Pallas kernels, give_back(): pl.pallas_call(back_kernel, out_shape=(jax.ShapeDtypeStruct((128, 1024),...  56.1 us
    all_to_all x2, blocking collectives, sent_and_summed(): lax.all_to_all(blocks, axis, split_axis=0, concat_axis=0, tiled=True)  29.5 us
    all_to_all x2, blocking collectives, sent_to_all(): return lax.all_to_all(copies, axis, split_axis=0, concat_axis=0, tiled=True)  29.4 us
    pallas_call x1, Pallas kernels, dispatch(): pl.pallas_call(dispatch_kernel, out_shape=(jax.ShapeDtypeStruct((128, 102...  24.6 us
    all_to_all x2, waiting for transfers between devices, sent_to_all(): return lax.all_to_all(copies, axis, split_axis=0, concat_axis=0, tiled=True)  18.7 us
    all_to_all x2, waiting for transfers between devices, sent_and_summed(): lax.all_to_all(blocks, axis, split_axis=0, concat_axis=0, tiled=True)  12.7 us
    all_to_all x2, starting transfers between devices, sent_and_summed(): lax.all_to_all(blocks, axis, split_axis=0, concat_axis=0, tiled=True)  10.6 us
    all_to_all x2, starting transfers between devices, sent_to_all(): return lax.all_to_all(copies, axis, split_axis=0, concat_axis=0, tiled=True)  9.85 us
  transfers between devices with their start and end apart: 4, of which 4 were waited for; matrix products, arithmetic and copies ran while one was open for 5% of the time, Pallas kernels for 0%

profile of v1, /device:TPU:8, one launch (start us, length us, event | category | flops | bytes accessed | tf_op | source)
XLA Modules:
  0.0 239.1 jit_solution(13868157941692275509)
XLA Ops:
  0.6 24.6 %dispatch.1 = (bf16[128,1024]{1,0:T(8,128)(2,1)}, f32[128,1024]{1,0:T(8,128)}, bf16[128,1024]{1,0:T(8,128)(2,1)}, f32[64,1,128]{2,1,0:T(1,128)}) custom-call(bf16[128,1024]{1,0:T(8,128)(2,1)} %features.3, s32[1,128]{1,0:T(1,128)} %bitcast.161, s32[1,128]{1,0:T(1,128)} %bitcast.163, bf16[2,1024,1024]{2,1,0:T(8,128)(2,1)} %weight_hbm.3), custom_call_target="tpu_custom_call" | custom-call | tf_op jit(solution)/shard_map/dispatch/pallas_call | solution.py:295
  25.2 1.1 fusion.35
  26.3 1.1 fusion.21
  27.4 1.1 broadcast_in_dim.85
  28.5 4.9 %all-to-all-start = ((bf16[4,128,1024]{2,1,0:T(8,128)(2,1)}), bf16[4,128,1024]{2,1,0:T(8,128)(2,1)S(1)}, u32[]{:S(2)}, u32[]{:S(2)}) async-start(bf16[4,128,1024]{2,1,0:T(8,128)(2,1)} %broadcast_in_dim.85), calls=%async_computation | async-start | bytes 2097152 | tf_op jit(solution)/shard_map/all_to_all | solution.py:24
  33.6 0.3 reduce-window.9
  34.5 12.0 %all-to-all-done = bf16[4,128,1024]{2,1,0:T(8,128)(2,1)S(1)} async-done(((bf16[4,128,1024]{2,1,0:T(8,128)(2,1)}), bf16[4,128,1024]{2,1,0:T(8,128)(2,1)S(1)}, u32[]{:S(2)}, u32[]{:S(2)}) %all-to-all-start) | async-done | bytes 1048608 | tf_op jit(solution)/shard_map/all_to_all | solution.py:24
  46.5 2.9 %fusion = bf16[4,512,256]{1,2,0:T(8,128)(2,1)S(1)} fusion(bf16[512,1024,1]{1,0,2:T(8,128)(2,1)S(1)} %bitcast.138, bf16[4,1024,256]{2,1,0:T(8,128)(2,1)} %param.27), kind=kOutput, calls=%fused_computation.13 | convolution fusion | flops 1074266112 | bytes 4194304 | tf_op jit(solution)/shard_map/rd,kdc->krc/dot_general | solution.py:623
  49.5 1.6 select_convert_fusion.2
  51.1 2.2 select_convert_fusion.1
  53.5 0.4 fusion.78
  54.2 0.4 copy-done.24
  54.6 0.5 convolution_convert_fusion
  55.1 16.2 %all_to_all.40 = bf16[4,128,1024]{2,1,0:T(8,128)(2,1)S(1)} all-to-all(bf16[4,128,1024]{2,1,0:T(8,128)(2,1)S(1)} %bitcast.145), channel_id=1, replica_groups=mesh['event'=8,'pack'=8,'tensor'=4] {'tensor'}, dimensions={0} | all-to-all | bytes 2097152 | tf_op jit(solution)/shard_map/all_to_all | solution.py:39
  71.8 0.7 copy-done.5
  72.7 15.9 %all_to_all.41 = bf16[4,128,1024]{2,1,0:T(8,128)(2,1)} all-to-all(bf16[4,128,1024]{2,1,0:T(8,128)(2,1)S(1)} %broadcast_in_dim.90), channel_id=1, replica_groups=mesh['event'=8,'pack'=8,'tensor'=4] {'tensor'}, dimensions={0} | all-to-all | bytes 2097152 | tf_op jit(solution)/shard_map/all_to_all | solution.py:24
  88.6 1.2 broadcast_in_dim.92
  89.8 4.9 %all-to-all-start.4 = ((bf16[4,128,1024]{2,1,0:T(8,128)(2,1)}), bf16[4,128,1024]{2,1,0:T(8,128)(2,1)S(1)}, u32[]{:S(2)}, u32[]{:S(2)}) async-start(bf16[4,128,1024]{2,1,0:T(8,128)(2,1)} %broadcast_in_dim.92), calls=%async_computation.4 | async-start | bytes 2097152 | tf_op jit(solution)/shard_map/all_to_all | solution.py:24
  94.8 3.8 %convolution_bitcast_fusion = f32[2,512,512]{2,1,0:T(8,128)} fusion(bf16[512,1024,1]{1,0,2:T(8,128)(2,1)} %bitcast.142, bf16[2,1024,512]{2,1,0:T(8,128)(2,1)S(1)} %copy-done), kind=kOutput, calls=%fused_computation.9 | convolution fusion | flops 1073741824 | bytes 5242880 | tf_op jit(solution)/shard_map/rd,kdf->krf/dot_general | solution.py:654
  98.6 6.7 %all-to-all-done.4 = bf16[4,128,1024]{2,1,0:T(8,128)(2,1)S(1)} async-done(((bf16[4,128,1024]{2,1,0:T(8,128)(2,1)}), bf16[4,128,1024]{2,1,0:T(8,128)(2,1)S(1)}, u32[]{:S(2)}, u32[]{:S(2)}) %all-to-all-start.4) | async-done | bytes 1048608 | tf_op jit(solution)/shard_map/all_to_all | solution.py:24
  105.3 2.9 %fusion.48 = (bf16[1,512,512]{2,1,0:T(8,128)(2,1)S(1)}, bf16[1,512,512]{2,1,0:T(8,128)(2,1)S(1)}) fusion(f32[2,512,512]{2,1,0:T(8,128)} %convolution_bitcast_fusion, bf16[512,1024]{1,0:T(8,128)(2,1)S(1)} %bitcast.140, bf16[512,1024]{1,0:T(8,128)(2,1)} %param.30), kind=kOutput, calls=%fused_computation.90 | convolution fusion | flops 540278784 | bytes 5242880 | tf_op jit(solution)/shard_map/dot_general | solution.py:670
  108.2 2.4 bitcast_convert_fusion.1
  110.5 4.9 %all-to-all-start.5 = ((bf16[4,128,1024]{2,1,0:T(8,128)(2,1)}), bf16[4,128,1024]{2,1,0:T(8,128)(2,1)S(1)}, u32[]{:S(2)}, u32[]{:S(2)}) async-start(bf16[4,128,1024]{2,1,0:T(8,128)(2,1)} %bitcast.141), calls=%async_computation.5 | async-start | bytes 2097152 | tf_op jit(solution)/shard_map/all_to_all | solution.py:39
  115.5 3.6 %convolution_convert_fusion.2 = bf16[512,1024]{1,0:T(8,128)(2,1)} fusion(bf16[512,1024]{1,0:T(8,128)(2,1)} %param.30, f32[2,512,512]{2,1,0:T(8,128)} %convolution_bitcast_fusion), kind=kOutput, calls=%fused_computation.12 | convolution fusion | flops 538968064 | bytes 4194304 | tf_op jit(solution)/shard_map/dot_general | solution.py:664
  119.1 5.8 %all-to-all-done.5 = bf16[4,128,1024]{2,1,0:T(8,128)(2,1)S(1)} async-done(((bf16[4,128,1024]{2,1,0:T(8,128)(2,1)}), bf16[4,128,1024]{2,1,0:T(8,128)(2,1)S(1)}, u32[]{:S(2)}, u32[]{:S(2)}) %all-to-all-start.5) | async-done | bytes 1048608 | tf_op jit(solution)/shard_map/all_to_all | solution.py:39
  124.9 1.0 copy-done.4
  125.9 5.7 %all-to-all-start.3 = ((bf16[4,128,1024]{2,1,0:T(8,128)(2,1)}), bf16[4,128,1024]{2,1,0:T(8,128)(2,1)}, u32[]{:S(2)}, u32[]{:S(2)}) async-start(bf16[4,128,1024]{2,1,0:T(8,128)(2,1)} %bitcast.139), calls=%async_computation.3 | async-start | bytes 2097152 | tf_op jit(solution)/shard_map/all_to_all | solution.py:39
  131.5 1.5 convert_reduce_fusion.1
  133.1 1.2 fusion.25
  134.2 6.9 %all-to-all-done.3 = bf16[4,128,1024]{2,1,0:T(8,128)(2,1)} async-done(((bf16[4,128,1024]{2,1,0:T(8,128)(2,1)}), bf16[4,128,1024]{2,1,0:T(8,128)(2,1)}, u32[]{:S(2)}, u32[]{:S(2)}) %all-to-all-start.3) | async-done | bytes 1048608 | tf_op jit(solution)/shard_map/all_to_all | solution.py:39
  141.1 1.5 convert_reduce_fusion.2
  142.6 1.0 fusion.29
  143.6 13.4 %all_to_all.42 = bf16[4,128,1024]{2,1,0:T(8,128)(2,1)S(1)} all-to-all(bf16[4,128,1024]{2,1,0:T(8,128)(2,1)S(1)} %broadcast_in_dim.93), channel_id=1, replica_groups=mesh['event'=8,'pack'=8,'tensor'=4] {'tensor'}, dimensions={0} | all-to-all | bytes 2097152 | tf_op jit(solution)/shard_map/all_to_all | solution.py:24
  157.1 1.7 divide_convert_fusion
  159.1 0.6 fusion.2
  159.7 0.3 copy-done.12
  160.5 0.3 copy-done.27
  160.9 1.2 select_convert_fusion
  162.1 0.3 fusion.5
  162.4 0.4 fusion.7
  162.8 0.3 fusion.4
  163.2 0.8 copy-done.23
  164.0 1.3 bitcast_convert_fusion
  165.3 13.3 %all_to_all.43 = bf16[4,128,1024]{2,1,0:T(8,128)(2,1)S(1)} all-to-all(bf16[4,128,1024]{2,1,0:T(8,128)(2,1)S(1)} %bitcast.144), channel_id=1, replica_groups=mesh['event'=8,'pack'=8,'tensor'=4] {'tensor'}, dimensions={0} | all-to-all | bytes 2097152 | tf_op jit(solution)/shard_map/all_to_all | solution.py:39
  179.0 1.0 fusion.34.d_quarter
  180.0 56.1 %give_back.1 = (bf16[128,1024]{1,0:T(8,128)(2,1)}, f32[2,16,256]{2,1,0:T(8,128)}) custom-call(bf16[128,1024]{1,0:T(8,128)(2,1)} %fusion.34.d_quarter, f32[64,1,128]{2,1,0:T(1,128)} %get-tuple-element.74.got_slots, s32[1,128]{1,0:T(1,128)} %bitcast.162, bf16[128,1024]{1,0:T(8,128)(2,1)} %features.3, bf16[128,1024]{1,0:T(8,128)(2,1)} %get-tuple-element.75.activation, ...), custom_call_target="tpu_custom_call" | custom-call | tf_op jit(solution)/shard_map/give_back/pallas_call | solution.py:564
  236.1 1.7 copy.21
  237.7 1.4 copy.22
  (79 shorter events, 3.3 us)
Async XLA Ops:
  0.6 94.1 %copy-start = (bf16[2,1024,512]{2,1,0:T(8,128)(2,1)S(1)}, bf16[2,1024,512]{2,1,0:T(8,128)(2,1)}, u32[]{:S(2)}) copy-start(bf16[2,1024,512]{2,1,0:T(8,128)(2,1)} %param.29) | copy-start | bytes 6291460
  25.2 8.2 %copy-start.22 = (s32[1,512]{1,0:T(1,128)S(1)}, s32[1,512]{1,0:T(1,128)}, u32[]{:S(2)}) copy-start(s32[1,512]{1,0:T(1,128)} %param.25) | copy-start | bytes 6148
  28.5 18.0 %all-to-all-start = ((bf16[4,128,1024]{2,1,0:T(8,128)(2,1)}), bf16[4,128,1024]{2,1,0:T(8,128)(2,1)S(1)}, u32[]{:S(2)}, u32[]{:S(2)}) async-start(bf16[4,128,1024]{2,1,0:T(8,128)(2,1)} %broadcast_in_dim.85), calls=%async_computation | async-start | bytes 2097152 | tf_op jit(solution)/shard_map/all_to_all | solution.py:24
  34.3 15.2 %copy-start.20 = (pred[256,256]{1,0:T(8,128)(4,1)}, pred[256,256]{1,0:T(8,128)(4,1)S(1)}, u32[]{:S(2)}) copy-start(pred[256,256]{1,0:T(8,128)(4,1)S(1)} %fusion.50) | copy-start | bytes 196612
  49.4 4.7 %copy-start.17 = (bf16[4,512,256]{1,2,0:T(8,128)(2,1)}, bf16[4,512,256]{1,2,0:T(8,128)(2,1)S(1)}, u32[]{:S(2)}) copy-start(bf16[4,512,256]{1,2,0:T(8,128)(2,1)S(1)} %fusion) | copy-start | bytes 3145732
  49.5 1.6 copy-start.11
  49.5 1.6 copy-start.15
  49.5 4.0 %copy-start.9 = (bf16[1,512,256]{1,2,0:T(8,128)(2,1)}, bf16[1,512,256]{1,2,0:T(8,128)(2,1)S(1)}, u32[]{:S(2)}) copy-start(bf16[1,512,256]{1,2,0:T(8,128)(2,1)S(1)} %get-tuple-element.85) | copy-start | bytes 786436
  51.1 2.2 copy-start.7
  53.2 1.0 copy-start.2
  53.2 1.4 copy-start.24
  54.6 16.7 %copy-start.18 = (f32[512,256]{0,1:T(8,128)}, f32[512,256]{0,1:T(8,128)S(1)}, u32[]{:S(2)}) copy-start(f32[512,256]{0,1:T(8,128)S(1)} %bitcast_divide_fusion) | copy-start | bytes 1572868
  55.1 16.4 %copy-start.1 = (bf16[128,1024]{1,0:T(8,128)(2,1)S(1)}, bf16[128,1024]{1,0:T(8,128)(2,1)}, u32[]{:S(2)}) copy-start(bf16[128,1024]{1,0:T(8,128)(2,1)} %get-tuple-element.73) | copy-start | bytes 786436
  71.7 0.7 copy-start.5
  71.7 16.9 %copy-start.13 = (bf16[1,128,1024]{2,1,0:T(8,128)(2,1)S(1)}, bf16[1,128,1024]{2,1,0:T(8,128)(2,1)}, u32[]{:S(2)}) copy-start(bf16[1,128,1024]{2,1,0:T(8,128)(2,1)} %param.31) | copy-start | bytes 786436
  89.8 15.4 %all-to-all-start.4 = ((bf16[4,128,1024]{2,1,0:T(8,128)(2,1)}), bf16[4,128,1024]{2,1,0:T(8,128)(2,1)S(1)}, u32[]{:S(2)}, u32[]{:S(2)}) async-start(bf16[4,128,1024]{2,1,0:T(8,128)(2,1)} %broadcast_in_dim.92), calls=%async_computation.4 | async-start | bytes 2097152 | tf_op jit(solution)/shard_map/all_to_all | solution.py:24
  110.5 14.4 %all-to-all-start.5 = ((bf16[4,128,1024]{2,1,0:T(8,128)(2,1)}), bf16[4,128,1024]{2,1,0:T(8,128)(2,1)S(1)}, u32[]{:S(2)}, u32[]{:S(2)}) async-start(bf16[4,128,1024]{2,1,0:T(8,128)(2,1)} %bitcast.141), calls=%async_computation.5 | async-start | bytes 2097152 | tf_op jit(solution)/shard_map/all_to_all | solution.py:39
  124.9 1.0 copy-start.4
  125.9 15.2 %all-to-all-start.3 = ((bf16[4,128,1024]{2,1,0:T(8,128)(2,1)}), bf16[4,128,1024]{2,1,0:T(8,128)(2,1)}, u32[]{:S(2)}, u32[]{:S(2)}) async-start(bf16[4,128,1024]{2,1,0:T(8,128)(2,1)} %bitcast.139), calls=%async_computation.3 | async-start | bytes 2097152 | tf_op jit(solution)/shard_map/all_to_all | solution.py:39
  131.5 11.0 %copy-start.6 = (bf16[128,1024]{1,0:T(8,128)(2,1)S(1)}, bf16[128,1024]{1,0:T(8,128)(2,1)}, u32[]{:S(2)}) copy-start(bf16[128,1024]{1,0:T(8,128)(2,1)} %copy-done.5) | copy-start | bytes 786436
  131.5 11.0 %copy-start.14 = (bf16[1,128,1024]{2,1,0:T(8,128)(2,1)S(1)}, bf16[1,128,1024]{2,1,0:T(8,128)(2,1)}, u32[]{:S(2)}) copy-start(bf16[1,128,1024]{2,1,0:T(8,128)(2,1)} %param.31) | copy-start | bytes 786436
  143.5 13.6 %copy-start.19 = (f32[512,256]{0,1:T(8,128)S(1)}, f32[512,256]{0,1:T(8,128)}, u32[]{:S(2)}) copy-start(f32[512,256]{0,1:T(8,128)} %copy-done.18) | copy-start | bytes 1572868
  143.5 13.6 %copy-start.25 = (bf16[256,1024]{1,0:T(8,128)(2,1)S(1)}, bf16[256,1024]{1,0:T(8,128)(2,1)}, u32[]{:S(2)}) copy-start(bf16[256,1024]{1,0:T(8,128)(2,1)} %param.28) | copy-start | bytes 1572868
  157.1 1.7 copy-start.8
  157.1 2.0 copy-start.10
  157.1 2.0 copy-start.21
  157.1 2.0 copy-start.26
  159.1 1.0 copy-start.12
  159.1 1.2 copy-start.16
  159.1 1.8 copy-start.27
  160.9 1.2 copy-start.3
  162.4 1.6 copy-start.23

commit v2 on v1

v2 whole, which is shorter than its diff:
```python
import jax
import jax.numpy as jnp
from jax import lax
from jax.experimental import pallas as pl
from jax.experimental.pallas import tpu as pltpu
from jax.sharding import PartitionSpec as P

MESH = pl.DeviceIdType.MESH
EPS = 1e-06
GROUPS = 64
CAP = 3
BLOCK_ROWS = CAP * 8
VMEM_LIMIT = 63 * 1024 * 1024
HEAD_SCALE = 64**-0.5


def silu_grad(value):
    sigma = jax.nn.sigmoid(value)
    return sigma * (1.0 + value * (1.0 - sigma))


def norm_rows(rows):
    factor = lax.rsqrt(jnp.mean(rows * rows, axis=-1, keepdims=True) + EPS)
    return (rows * factor, factor)


def norm_back(grad, normed, factor):
    return factor * (grad - normed * jnp.mean(grad * normed, axis=-1, keepdims=True))


def where_am_i():
    return (lax.axis_index("event"), lax.axis_index("pack"), lax.axis_index("tensor"))


def peer(index, tensor):
    return (index // 8, lax.rem(index, 8), tensor)


def greet_all(barrier, me, tensor):
    def greet(step, carry):
        pl.semaphore_signal(
            barrier, inc=1, device_id=peer(lax.rem(me + step, GROUPS), tensor), device_id_type=MESH
        )
        return carry

    lax.fori_loop(1, GROUPS, greet, 0)


def exchange_copy(source, target, me, tensor, step, send_sem, recv_sem):
    other = lax.rem(me + step, GROUPS)
    return pltpu.make_async_remote_copy(
        src_ref=source.at[other],
        dst_ref=target.at[me],
        send_sem=send_sem,
        recv_sem=recv_sem,
        device_id=peer(other, tensor),
        device_id_type=MESH,
    )


def start_exchange(source, target, me, tensor, send_sem, recv_sem):
    def start(step, carry):
        exchange_copy(source, target, me, tensor, step, send_sem, recv_sem).start()
        return carry

    lax.fori_loop(1, GROUPS, start, 0)
    target[me] = source[me]


def await_bytes(ref, sem):
    pltpu.make_async_copy(ref, ref, sem).wait()


def end_exchange(source, target, send_sem, recv_sem):
    await_bytes(source.at[pl.ds(0, GROUPS - 1)], send_sem)
    await_bytes(target.at[pl.ds(0, GROUPS - 1)], recv_sem)


def dot32(left, right, dims=((1,), (0,))):
    return lax.dot_general(left, right, (dims, ((), ())), preferred_element_type=jnp.float32)


def routing(owner_row):
    rows = jnp.broadcast_to(owner_row, (128, 128))
    columns = rows.T
    earlier = lax.broadcasted_iota(jnp.int32, (128, 128), 0) < lax.broadcasted_iota(
        jnp.int32, (128, 128), 1
    )
    rank = jnp.sum(jnp.where((columns == rows) & earlier, 1.0, 0.0), axis=0, keepdims=True)
    group = lax.broadcasted_iota(jnp.int32, (GROUPS, 128), 0).astype(jnp.float32)
    mine = owner_row == group
    return [mine & (rank == float(k)) for k in range(CAP)]


def one_hot(mask):
    return jnp.where(mask, 1.0, 0.0).astype(jnp.bfloat16)


def spread_rows(wide, k, rows):
    for part in range(8):
        wide[pl.ds(k * 8 + part, GROUPS, stride=BLOCK_ROWS), :] = rows[
            :, part * 128 : (part + 1) * 128
        ]


def joined_rows(wide, k):
    return jnp.concatenate(
        [wide[pl.ds(k * 8 + part, GROUPS, stride=BLOCK_ROWS), :] for part in range(8)], axis=1
    ).astype(jnp.bfloat16)


def silu(value):
    return value * jax.nn.sigmoid(value)


class Halving:
    def __init__(self, blocks, first, second, outgoing, sems, base, index, device):
        self.blocks, self.first, self.second, self.outgoing = blocks, first, second, outgoing
        self.sems, self.base, self.index = sems, base, index
        near = index + 1 - 2 * lax.rem(index, 2)
        self.other = (near, 3 - index)
        self.far = lax.rem(index + 2, 4)
        self.device = device

    def copy(self, source, target, number, half_partner):
        send, recv = self.sems
        return pltpu.make_async_remote_copy(
            src_ref=source,
            dst_ref=target,
            send_sem=send.at[self.base + number],
            recv_sem=recv.at[self.base + number],
            device_id=self.device(half_partner),
            device_id_type=MESH,
        )

    def round_one(self):
        copies = []
        for half in range(2):
            partner = self.other[half]
            for slot, block in enumerate((partner, self.far)):
                copies.append(
                    self.copy(
                        self.blocks.at[block, half],
                        self.first.at[half, slot],
                        half * 2 + slot,
                        partner,
                    )
                )
        return copies

    def round_two(self):
        return [
            self.copy(self.outgoing.at[half], self.second.at[half], 4 + half, self.other[1 - half])
            for half in range(2)
        ]

    def start_one(self):
        for copy in self.round_one():
            copy.start()

    def start_two(self):
        for copy in self.round_one():
            copy.wait()
        for half in range(2):
            block = self.other[1 - half]
            self.outgoing[half] = (
                self.blocks[block, half].astype(jnp.float32)
                + self.first[half, 1].astype(jnp.float32)
            ).astype(jnp.bfloat16)
        for copy in self.round_two():
            copy.start()

    def finish(self):
        for copy in self.round_two():
            copy.wait()
        return [
            (
                self.blocks[self.index, half].astype(jnp.float32)
                + self.first[half, 0].astype(jnp.float32)
                + self.second[half].astype(jnp.float32)
            ).astype(jnp.bfloat16)
            for half in range(2)
        ]


class Gather:
    def __init__(self, send, recv, event, pack, tensor):
        self.send, self.recv = send, recv
        self.event, self.pack, self.tensor = event, pack, tensor
        self.core = lax.rem(event, 2)
        self.used = 0
        self.started = []
        self.partner = (event + 1 - 2 * self.core, pack, tensor)
        self.pair_started = []

    def copy(self, source, target, device):
        number = self.used
        self.used += 1
        copy = pltpu.make_async_remote_copy(
            src_ref=source,
            dst_ref=target,
            send_sem=self.send.at[number],
            recv_sem=self.recv.at[number],
            device_id=device,
            device_id_type=MESH,
        )
        copy.start()
        self.started.append(copy)
        return copy

    def along_tensor(self, shift):
        return (self.event, self.pack, lax.rem(self.tensor + shift + 4, 4))

    def along_x(self, shift):
        return (lax.rem(self.event + 2 * shift + 8, 8), self.pack, self.tensor)

    def along_z(self, shift):
        return (self.event, lax.rem(self.pack + shift + 8, 8), self.tensor)

    def to_pair(self, region):
        self.pair_started.append(self.copy(region, region, self.partner))

    def end(self):
        for copy in self.started:
            copy.wait_send()
        for copy in self.pair_started:
            copy.wait_recv()


class TensorRing:
    def __init__(self, gather, own, region, halves):
        self.gather, self.own, self.region, self.halves = gather, own, region, halves

    def start(self):
        device = self.gather.along_tensor
        self.near = [
            self.gather.copy(self.own, self.region(2), device(1)),
            self.gather.copy(self.own, self.region(1), device(-1)),
        ]

    def relay(self):
        for copy in self.near:
            copy.wait_recv()
        device = self.gather.along_tensor
        plus, minus = self.halves
        self.far = [self.gather.copy(self.region(2, plus), self.region(3, plus), device(1))]
        if minus is not None:
            self.far.append(
                self.gather.copy(self.region(1, minus), self.region(3, minus), device(-1))
            )

    def end(self):
        for copy in self.far:
            copy.wait_recv()
        self.gather.to_pair(self.region(pl.ds(1, 3)))


class SideRing:
    def __init__(self, gather, size, index, device, region, halves):
        self.gather, self.size, self.index = gather, size, index
        self.device, self.region, self.halves = device, region, halves
        self.step = 0
        self.flying = None

    def block(self, shift, half=None):
        return self.region(lax.rem(self.index + shift + self.size, self.size), half)

    def start(self):
        block = self.block(0)
        self.flying = [
            self.gather.copy(block, block, self.device(1)),
            self.gather.copy(block, block, self.device(-1)),
        ]
        self.step = 1

    def advance(self):
        for copy in self.flying:
            copy.wait_recv()
        step = self.step
        last = step == self.size // 2
        forward = []
        if not last:
            halves = (None, None) if step + 1 < self.size // 2 else self.halves
            for sign, half in zip((1, -1), halves):
                if half is not False:
                    block = self.block(-sign * step, half)
                    forward.append(self.gather.copy(block, block, self.device(sign)))
            for sign in (1, -1):
                self.gather.to_pair(self.block(-sign * step))
        else:
            self.gather.to_pair(self.block(step))
        self.flying = forward
        self.step = step + 1


def masks(documents, tensor):
    own = documents[:, pl.ds(pl.multiple_of(tensor * 128, 128), 128)].astype(jnp.float32)
    before = documents[
        :, pl.ds(pl.multiple_of(lax.rem(tensor + 3, 4) * 128, 128), 128)
    ].astype(jnp.float32)
    before = before - jnp.where(tensor == 0, 1000.0, 0.0)
    mine = jnp.broadcast_to(own, (128, 128)).T
    row = lax.broadcasted_iota(jnp.int32, (128, 128), 0)
    column = lax.broadcasted_iota(jnp.int32, (128, 128), 1)
    allowed = jnp.concatenate(
        [
            jnp.where(mine == before, 1.0, 0.0),
            jnp.where((mine == own) & (column <= row), 1.0, 0.0),
        ],
        axis=1,
    )
    root = jnp.sqrt(jnp.sum(allowed, axis=1, keepdims=True))
    return (allowed, root)


def by_parity(value):
    first = lax.rem(lax.broadcasted_iota(jnp.int32, value.shape, 1), 128) < 64
    return (
        jnp.where(first, value, 0.0).astype(jnp.bfloat16),
        jnp.where(first, 0.0, value).astype(jnp.bfloat16),
    )


def rounded(value):
    return value.astype(jnp.bfloat16).astype(jnp.float32)


def step_kernel(
    features,
    owner,
    slot,
    documents,
    out_grad,
    enc_hbm,
    attn_in_hbm,
    attn_out_hbm,
    ffn_in_hbm,
    ffn_out_hbm,
    packed_out,
    row_grad,
    enc_grad,
    enc,
    attn_in,
    attn_out,
    ffn_in,
    ffn_out,
    preact,
    wide,
    send_rows,
    got_rows,
    send_slots,
    got_slots,
    back_rows,
    acts,
    cots,
    grads,
    firsts,
    seconds,
    outs,
    grads2,
    firsts2,
    seconds2,
    outs2,
    send_z,
    got_z,
    normed,
    query,
    keys,
    values,
    gates,
    attended,
    weights,
    slopes,
    total_a,
    total_b,
    residual,
    normed2,
    allowed_ref,
    root_ref,
    halo_send,
    halo_got,
    load_sem,
    send_sem,
    recv_sem,
    ready_sem,
    gather_send,
    gather_recv,
    pair_send,
    pair_recv,
    half_send,
    half_recv,
    z_send,
    z_recv,
    halo_sem,
):
    event, pack, tensor = where_am_i()
    me = event * 8 + pack
    core = lax.rem(event, 2)
    chip_x = event // 2
    partner = (event + 1 - 2 * core, pack, tensor)
    bf16, f32 = jnp.bfloat16, jnp.float32
    barrier = pltpu.get_barrier_semaphore()
    loads = []
    for number, (source, target) in enumerate(
        (
            (enc_hbm.at[0], enc.at[0]),
            (enc_hbm.at[1], enc.at[1]),
            (attn_in_hbm, attn_in.at[0]),
            (attn_out_hbm, attn_out.at[0]),
            (ffn_in_hbm, ffn_in.at[0]),
            (ffn_out_hbm, ffn_out.at[0]),
        )
    ):
        load = pltpu.make_async_copy(source, target, load_sem.at[number])
        load.start()
        loads.append(load)
    for step in range(1, 8):
        for device in (
            (event, lax.rem(pack + step, 8), tensor),
            (lax.rem(event + step, 8), pack, tensor),
        ):
            pl.semaphore_signal(barrier, inc=1, device_id=device, device_id_type=MESH)
    for step in (1, 3):
        pl.semaphore_signal(
            barrier,
            inc=1,
            device_id=(event, pack, lax.rem(tensor + step, 4)),
            device_id_type=MESH,
        )
    picks = routing(owner[...].astype(f32))
    slot_row = slot[...].astype(f32) + 1.0
    lane = lax.broadcasted_iota(jnp.int32, (GROUPS, 128), 1)
    slots = jnp.full((GROUPS, 128), -1.0, f32)
    for k in range(CAP):
        value = jnp.sum(jnp.where(picks[k], slot_row, 0.0), axis=1, keepdims=True) - 1.0
        slots = jnp.where(lane == k, value, slots)
    send_slots[:, 0, :] = slots
    pl.semaphore_wait(barrier, 16)
    for step in range(1, 8):
        pl.semaphore_signal(
            ready_sem,
            inc=1,
            device_id=(lax.rem(event + step, 8), pack, tensor),
            device_id_type=MESH,
        )

    gather = Gather(gather_send, gather_recv, event, pack, tensor)
    both = (pl.ds(0, 2), pl.ds(2, 2))

    def part_a(where, half=None):
        return attn_in.at[where, slice(None) if half is None else half, chip_x, core]

    def part_o(where, half=None):
        return attn_out.at[where, pack, core]

    def part_i(where, half=None):
        return ffn_in.at[where, slice(None) if half is None else half, core]

    def part_f(where, half=None):
        return ffn_out.at[where, pack, core, slice(None) if half is None else half]

    ring_f = TensorRing(gather, ffn_out_hbm.at[pack, core], part_f, (pl.ds(0, 1), pl.ds(1, 1)))
    ring_o = TensorRing(gather, attn_out_hbm.at[pack, core], part_o, (None, None))
    ring_a = TensorRing(gather, attn_in_hbm.at[:, chip_x, core], part_a, both)
    ring_i = TensorRing(gather, ffn_in_hbm.at[:, core], part_i, (pl.ds(0, 1), pl.ds(1, 1)))
    foreign = pl.ds(1, 3)

    def side_a(index, half=None):
        return attn_in.at[foreign, slice(None) if half is None else half, index, core]

    def side_o(index, half=None):
        return attn_out.at[foreign, index, core]

    def side_f(index, half=None):
        return ffn_out.at[foreign, index, core, slice(None) if half is None else half]

    x_a = SideRing(gather, 4, chip_x, gather.along_x, side_a, both)
    z_o = SideRing(gather, 8, pack, gather.along_z, side_o, (None, False))
    z_f = SideRing(gather, 8, pack, gather.along_z, side_f, (pl.ds(0, 1), pl.ds(1, 1)))

    ring_f.start()
    ring_o.start()
    loads[0].wait()
    acts[0, 0] = features[...]
    pre = dot32(features[...], enc[0])
    preact[...] = pre
    act = silu(pre).astype(bf16)
    acts[1, 0] = act
    ring_f.relay()
    ring_o.relay()
    ring_a.start()
    loads[1].wait()
    encoded = dot32(act, enc[1]).astype(bf16)
    ring_f.end()
    ring_o.end()
    z_f.start()
    z_o.start()
    for k in range(CAP):
        spread_rows(wide, k, dot32(one_hot(picks[k]), encoded))
    send_rows[...] = wide[...].astype(bf16).reshape(GROUPS, BLOCK_ROWS, 128)
    pl.semaphore_wait(ready_sem, 7)
    start_exchange(send_slots, got_slots, me, tensor, send_sem.at[0], recv_sem.at[0])
    start_exchange(send_rows, got_rows, me, tensor, send_sem.at[1], recv_sem.at[1])
    ring_a.relay()
    ring_i.start()
    ring_a.end()
    x_a.start()
    z_f.advance()
    z_o.advance()

    def pair_copy(number, array):
        return pltpu.make_async_remote_copy(
            src_ref=array.at[0],
            dst_ref=array.at[1],
            send_sem=pair_send.at[number],
            recv_sem=pair_recv.at[number],
            device_id=partner,
            device_id_type=MESH,
        )

    act_copies = [pair_copy(layer, acts.at[layer]) for layer in range(2)]
    for copy in act_copies:
        copy.start()
    end_exchange(send_slots, got_slots, send_sem.at[0], recv_sem.at[0])
    end_exchange(send_rows, got_rows, send_sem.at[1], recv_sem.at[1])
    wide[...] = got_rows[...].reshape(GROUPS * BLOCK_ROWS, 128).astype(f32)
    turned = jnp.concatenate([got_slots[:, 0, :], jnp.full((GROUPS, 128), -1.0, f32)], axis=0).T
    place = lax.broadcasted_iota(jnp.int32, (128, GROUPS), 0).astype(f32)
    total = None
    for k in range(CAP):
        pick = one_hot(turned[k : k + 1, :GROUPS] == place)
        term = dot32(pick, joined_rows(wide, k))
        total = term if total is None else total + term
    quarter = total
    normed_f, factor1 = norm_rows(quarter)
    halo_send[0] = normed_f.astype(bf16)
    normed[1] = normed_f.astype(bf16)
    residual[...] = quarter

    def halo_copy(number, target, shift):
        return pltpu.make_async_remote_copy(
            src_ref=halo_send.at[number],
            dst_ref=target,
            send_sem=halo_sem.at[number],
            recv_sem=halo_sem.at[2 + number],
            device_id=(event, pack, lax.rem(tensor + shift, 4)),
            device_id_type=MESH,
        )

    halo = halo_copy(0, normed.at[0], 1)
    halo.start()
    allowed, root = masks(documents, tensor)
    allowed_ref[...] = allowed
    root_ref[...] = jnp.broadcast_to(root, (128, 128))
    z_f.advance()
    z_o.advance()
    x_a.advance()
    z_f.advance()
    z_o.advance()
    ring_i.relay()
    z_f.advance()
    z_o.advance()
    x_a.advance()
    ring_i.end()
    gather.end()
    for load in loads[2:]:
        load.wait()
    halo.wait()
    own_rows = normed[1]
    all_rows = normed[...].reshape(256, 1024)
    total_a[...] = quarter

    def attend(slot_index, carry):
        def matrix(number):
            return attn_in[slot_index, number].reshape(1024, 256)

        query_f = rounded(dot32(own_rows, matrix(0)))
        gate = rounded(dot32(own_rows, matrix(3)))
        keys_f = rounded(dot32(all_rows, matrix(1)))
        values_f = rounded(dot32(all_rows, matrix(2)))
        gates[slot_index] = gate
        sides = []
        for ref, value in ((query, query_f), (keys, keys_f), (values, values_f)):
            pieces = by_parity(value)
            for parity in range(2):
                ref[slot_index, parity] = pieces[parity]
            sides.append(pieces)
        parts = []
        allowed = allowed_ref[...] > 0.5
        for pair in range(2):
            columns = slice(pair * 128, (pair + 1) * 128)
            part = None
            for parity in range(2):
                scores = (
                    dot32(sides[0][parity][:, columns], sides[1][parity][:, columns], ((1,), (1,)))
                    * HEAD_SCALE
                )
                sigma = jax.nn.sigmoid(scores)
                weight = jnp.where(allowed, scores * sigma, 0.0).astype(bf16)
                weights[slot_index, pair * 2 + parity] = weight
                slopes[slot_index, pair * 2 + parity] = jnp.where(
                    allowed, sigma * (1.0 + scores * (1.0 - sigma)), 0.0
                )
                term = dot32(weight, sides[2][parity][:, columns])
                part = term if part is None else part + term
            parts.append(part)
        result = jnp.concatenate(parts, axis=1) / root_ref[:, 0:1]
        attended[slot_index] = result
        gated = (result * silu(gate)).astype(bf16)
        total_a[...] += rounded(dot32(gated, attn_out[slot_index].reshape(256, 1024)))
        return carry

    lax.fori_loop(0, 4, attend, 0)
    resid = rounded(total_a[...])
    normed2_f, factor2 = norm_rows(resid)
    normed2[...] = normed2_f.astype(bf16)
    total_a[...] = resid
    total_b[...] = jnp.zeros((128, 1024), f32)

    def feed(slot_index, carry):
        rows = normed2[...]
        gate = dot32(rows, ffn_in[slot_index, 0].reshape(1024, 512))
        upper = dot32(rows, ffn_in[slot_index, 1].reshape(1024, 512))
        sigma = jax.nn.sigmoid(gate)
        active = gate * sigma
        down = ffn_out[slot_index].reshape(512, 1024)
        total_a[...] += rounded(dot32((active * upper).astype(bf16), down))
        d_hidden = dot32(out_grad[...], down, ((1,), (1,)))
        d_gate = (d_hidden * upper * (sigma * (1.0 + gate * (1.0 - sigma)))).astype(bf16)
        d_upper = (d_hidden * active).astype(bf16)
        total_b[...] += rounded(
            dot32(d_gate, ffn_in[slot_index, 0].reshape(1024, 512), ((1,), (1,)))
            + dot32(d_upper, ffn_in[slot_index, 1].reshape(1024, 512), ((1,), (1,)))
        )
        return carry

    lax.fori_loop(0, 4, feed, 0)
    packed_out[...] = total_a[...].astype(bf16)
    d_resid = (
        out_grad[...].astype(f32) + norm_back(total_b[...], normed2_f, factor2)
    ).astype(bf16)
    total_a[...] = jnp.zeros((128, 1024), f32)
    total_b[...] = jnp.zeros((128, 1024), f32)

    def attend_back(slot_index, carry):
        gate = gates[slot_index]
        d_gated = dot32(d_resid, attn_out[slot_index].reshape(256, 1024), ((1,), (1,)))
        sigma = jax.nn.sigmoid(gate)
        d_attended = by_parity(d_gated * (gate * sigma) / root_ref[:, 0:1])
        d_gate = (
            d_gated * attended[slot_index] * (sigma * (1.0 + gate * (1.0 - sigma)))
        ).astype(bf16)
        d_parts = [[], [], []]
        for pair in range(2):
            columns = slice(pair * 128, (pair + 1) * 128)
            sums = [None, None, None]
            for parity in range(2):
                head = pair * 2 + parity
                d_side = d_attended[parity][:, columns]
                d_weights = dot32(d_side, values[slot_index, parity, :, columns], ((1,), (1,)))
                d_scores = (d_weights * slopes[slot_index, head]).astype(bf16)
                terms = (
                    dot32(d_scores, keys[slot_index, parity, :, columns]),
                    dot32(d_scores, query[slot_index, parity, :, columns], ((0,), (0,))),
                    dot32(weights[slot_index, head], d_side, ((0,), (0,))),
                )
                for number, term in enumerate(terms):
                    sums[number] = term if sums[number] is None else sums[number] + term
            d_parts[0].append(sums[0] * HEAD_SCALE)
            d_parts[1].append(sums[1] * HEAD_SCALE)
            d_parts[2].append(sums[2])
        d_query, d_keys, d_values = (
            jnp.concatenate(parts, axis=1).astype(bf16) for parts in d_parts
        )
        keys_back = dot32(d_keys, attn_in[slot_index, 1].reshape(1024, 256), ((1,), (1,)))
        values_back = dot32(d_values, attn_in[slot_index, 2].reshape(1024, 256), ((1,), (1,)))
        both_back = keys_back + values_back
        total_b[...] += both_back[:128]
        total_a[...] += (
            both_back[128:]
            + dot32(d_query, attn_in[slot_index, 0].reshape(1024, 256), ((1,), (1,)))
            + dot32(d_gate, attn_in[slot_index, 3].reshape(1024, 256), ((1,), (1,)))
        )
        return carry

    lax.fori_loop(0, 4, attend_back, 0)
    halo_send[1] = total_b[...].astype(bf16)
    halo_back = halo_copy(1, halo_got, 3)
    halo_back.start()
    halo_back.wait()
    d_normed = total_a[...] + halo_got[...].astype(f32)
    normed_f, factor1 = norm_rows(residual[...])
    d_quarter = (d_resid.astype(f32) + norm_back(d_normed, normed_f, factor1)).astype(bf16)
    lane = lax.broadcasted_iota(jnp.int32, (GROUPS, 128), 1).astype(jnp.float32)
    for k in range(CAP):
        pick = one_hot(got_slots[:, 0, k : k + 1] == lane)
        spread_rows(wide, k, dot32(pick, d_quarter))
    send_rows[...] = wide[...].astype(jnp.bfloat16).reshape(GROUPS, BLOCK_ROWS, 128)
    start_exchange(send_rows, back_rows, me, tensor, send_sem.at[2], recv_sem.at[2])
    picks = routing(owner[...].astype(jnp.float32))
    for copy in act_copies:
        copy.wait()
    end_exchange(send_rows, back_rows, send_sem.at[2], recv_sem.at[2])
    wide[...] = back_rows[...].reshape(GROUPS * BLOCK_ROWS, 128).astype(jnp.float32)
    total = None
    for k in range(CAP):
        term = dot32(one_hot(picks[k]), joined_rows(wide, k), ((0,), (0,)))
        total = term if total is None else total + term
    cotangent = total.astype(jnp.bfloat16)
    row_grad[...] = cotangent
    cots[1, 0] = cotangent
    cot_copies = [pair_copy(2 + layer, cots.at[layer]) for layer in range(2)]
    cot_copies[1].start()
    pre = preact[...]
    sigma = jax.nn.sigmoid(pre)
    back = dot32(cotangent, enc[1], ((1,), (1,)))
    cots[0, 0] = (back * (sigma * (1.0 + pre * (1.0 - sigma)))).astype(jnp.bfloat16)
    cot_copies[0].start()

    def tensor_device(index):
        return (event, pack, index)

    def chip_device(index):
        return (index * 2 + core, pack, tensor)

    rings = ((chip_x, chip_device), (tensor, tensor_device))
    stages = [[], []]
    for layer in range(2):
        for stage, refs in enumerate(
            ((grads, firsts, seconds, outs), (grads2, firsts2, seconds2, outs2))
        ):
            index, device = rings[layer] if stage == 0 else rings[1 - layer]
            stages[stage].append(
                Halving(
                    *(ref.at[layer] for ref in refs),
                    (half_send, half_recv),
                    (stage * 2 + layer) * 6,
                    index,
                    device,
                )
            )
    for layer in (1, 0):
        cot_copies[layer].wait()
        cot = cots[layer].reshape(256, 1024)
        for chip in range(4):
            columns = pl.ds(pl.multiple_of((chip * 2 + core) * 128, 128), 128)
            act = acts[layer, :, :, columns].reshape(256, 128)
            term = dot32(act, cot, ((0,), (0,))).astype(jnp.bfloat16)
            for block in range(4):
                for half in range(2):
                    piece = term[half * 64 : (half + 1) * 64, block * 256 : (block + 1) * 256]
                    if layer == 1:
                        grads[layer, block, half, chip] = piece
                    else:
                        grads[layer, chip, half, block] = piece
        stages[0][layer].start_one()
    for layer in (1, 0):
        stages[0][layer].start_two()
    for layer in (1, 0):
        for half, value in enumerate(stages[0][layer].finish()):
            for block in range(4):
                grads2[layer, block, half] = value[block]
        stages[1][layer].start_one()
    for layer in (1, 0):
        stages[1][layer].start_two()
    for layer in (1, 0):
        for half, value in enumerate(stages[1][layer].finish()):
            for quarter in range(4):
                send_z[half * 4 + quarter, layer] = value[quarter * 16 : (quarter + 1) * 16]
    z_copies = []
    for step in (1, 7, 2, 6, 3, 5, 4):
        other = lax.rem(pack + step, 8)
        z_copies.append(
            pltpu.make_async_remote_copy(
                src_ref=send_z.at[other],
                dst_ref=got_z.at[pack],
                send_sem=z_send.at[step],
                recv_sem=z_recv.at[step],
                device_id=(event, other, tensor),
                device_id_type=MESH,
            )
        )
        z_copies[-1].start()
    got_z[pack] = send_z[pack]
    for copy in z_copies:
        copy.wait()
    total = got_z[0].astype(jnp.float32)
    for source in range(1, 8):
        total = total + got_z[source].astype(jnp.float32)
    enc_grad[...] = total


def shards(
    features,
    dest_owner,
    dest_slot,
    doc_ids,
    enc_weight,
    attn_in,
    attn_out,
    ffn_in,
    ffn_out,
    out_grad,
):
    bf16, f32 = jnp.bfloat16, jnp.float32
    vmem = pl.BlockSpec(memory_space=pltpu.VMEM)
    hbm = pl.BlockSpec(memory_space=pl.ANY)
    dma = pltpu.SemaphoreType.DMA
    packed_out, row_grad, enc_grad = pl.pallas_call(
        step_kernel,
        out_shape=(
            jax.ShapeDtypeStruct((128, 1024), bf16),
            jax.ShapeDtypeStruct((128, 1024), bf16),
            jax.ShapeDtypeStruct((2, 16, 256), f32),
        ),
        in_specs=[vmem] * 5 + [hbm] * 5,
        out_specs=(vmem, vmem, vmem),
        scratch_shapes=[
            pltpu.VMEM((2, 1024, 1024), bf16),
            pltpu.VMEM((4, 4, 4, 2, 128, 256), bf16),
            pltpu.VMEM((4, 8, 2, 16, 1024), bf16),
            pltpu.VMEM((4, 2, 2, 512, 512), bf16),
            pltpu.VMEM((4, 8, 2, 2, 16, 1024), bf16),
            pltpu.VMEM((128, 1024), f32),
            pltpu.VMEM((GROUPS * BLOCK_ROWS, 128), f32),
            pltpu.VMEM((GROUPS, BLOCK_ROWS, 128), bf16),
            pltpu.VMEM((GROUPS, BLOCK_ROWS, 128), bf16),
            pltpu.VMEM((GROUPS, 1, 128), f32),
            pltpu.VMEM((GROUPS, 1, 128), f32),
            pltpu.VMEM((GROUPS, BLOCK_ROWS, 128), bf16),
            pltpu.VMEM((2, 2, 128, 1024), bf16),
            pltpu.VMEM((2, 2, 128, 1024), bf16),
            pltpu.VMEM((2, 4, 2, 4, 64, 256), bf16),
            pltpu.VMEM((2, 2, 2, 4, 64, 256), bf16),
            pltpu.VMEM((2, 2, 4, 64, 256), bf16),
            pltpu.VMEM((2, 2, 4, 64, 256), bf16),
            pltpu.VMEM((2, 4, 2, 64, 256), bf16),
            pltpu.VMEM((2, 2, 2, 64, 256), bf16),
            pltpu.VMEM((2, 2, 64, 256), bf16),
            pltpu.VMEM((2, 2, 64, 256), bf16),
            pltpu.VMEM((8, 2, 16, 256), bf16),
            pltpu.VMEM((8, 2, 16, 256), bf16),
            pltpu.VMEM((2, 128, 1024), bf16),
            pltpu.VMEM((4, 2, 128, 256), bf16),
            pltpu.VMEM((4, 2, 256, 256), bf16),
            pltpu.VMEM((4, 2, 256, 256), bf16),
            pltpu.VMEM((4, 128, 256), f32),
            pltpu.VMEM((4, 128, 256), f32),
            pltpu.VMEM((4, 4, 128, 256), bf16),
            pltpu.VMEM((4, 4, 128, 256), f32),
            pltpu.VMEM((128, 1024), f32),
            pltpu.VMEM((128, 1024), f32),
            pltpu.VMEM((128, 1024), f32),
            pltpu.VMEM((128, 1024), bf16),
            pltpu.VMEM((128, 256), f32),
            pltpu.VMEM((128, 128), f32),
            pltpu.VMEM((2, 128, 1024), bf16),
            pltpu.VMEM((128, 1024), bf16),
            dma((6,)),
            dma((3,)),
            dma((3,)),
            pltpu.SemaphoreType.REGULAR,
            dma((64,)),
            dma((64,)),
            dma((4,)),
            dma((4,)),
            dma((24,)),
            dma((24,)),
            dma((8,)),
            dma((8,)),
            dma((4,)),
        ],
        compiler_params=pltpu.CompilerParams(
            collective_id=0, has_side_effects=True, vmem_limit_bytes=VMEM_LIMIT
        ),
        name="train_step",
    )(
        features,
        dest_owner.reshape(1, 128),
        dest_slot.reshape(1, 128),
        doc_ids,
        out_grad[0],
        enc_weight,
        attn_in.reshape(4, 4, 2, 128, 256),
        attn_out.reshape(8, 2, 16, 1024),
        ffn_in.reshape(2, 2, 512, 512),
        ffn_out.reshape(8, 2, 2, 16, 1024),
    )
    return (packed_out[None], row_grad, enc_grad)


def solution(mesh):
    placed = (
        P(("event", "pack", "tensor"), None),
        P(("event", "pack", "tensor")),
        P(("event", "pack", "tensor")),
        P(("event", "pack"), None),
        P(),
        P(None, None, "tensor"),
        P("tensor", None),
        P(None, None, "tensor"),
        P("tensor", None),
        P(("event", "pack"), "tensor", None),
    )
    return jax.shard_map(
        shards,
        mesh=mesh,
        in_specs=placed,
        out_specs=(
            P(("event", "pack"), "tensor", None),
            P(("event", "pack", "tensor"), None),
            P(None, ("event", "pack"), "tensor"),
        ),
        check_vma=False,
    )
```

time: 241 us -> 149 us (0.62)
  Pallas kernels: 80.7 us -> 143 us
  blocking collectives: 58.9 us -> 0 us
  waiting for transfers between devices: 31.3 us -> 0 us
  matrix products: 26.9 us -> 0 us
  starting transfers between devices: 20.4 us -> 0 us
  other arithmetic: 10.1 us -> 0 us
  local copies, waits for them, and re-layouts: 9.65 us -> 4.71 us
    pallas_call x2 -> x1, Pallas kernels: 80.7 us -> 143 us  [shards(): pl.pallas_call(step_kernel, out_shape=(jax.ShapeDtypeStruct((128, 1024),...]
    all_to_all x4 -> x0, blocking collectives: 58.9 us -> none  [the longest x2 29.5 us: sent_and_summed(): lax.all_to_all(blocks, axis, split_axis=0, concat_axis=0, tiled=True)]
    all_to_all x4 -> x0, waiting for transfers between devices: 31.3 us -> none  [the longest x2 18.7 us: sent_to_all(): return lax.all_to_all(copies, axis, split_axis=0, concat_axis=0, tiled=True)]
    dot_general x20 -> x0, matrix products: 26.9 us -> none  [the longest x1 3.8 us: shards(): jnp.einsum('rd,kdf->krf', gather_directly(normed2, 'tensor', 0), ffn_in,...]
    all_to_all x4 -> x0, starting transfers between devices: 20.4 us -> none  [the longest x2 10.6 us: sent_and_summed(): lax.all_to_all(blocks, axis, split_axis=0, concat_axis=0, tiled=True)]
    reduce_sum x8 -> x0, other arithmetic: 5.97 us -> none  [the longest x4 3.34 us: sent_and_summed(): return arrived.astype(jnp.float32).sum(axis=0)]
    convert_element_type x4 -> x0, other arithmetic: 3.09 us -> none  [the longest x1 1.07 us: shards(): normed = normed_f.astype(jnp.bfloat16)]
    broadcast_in_dim x4 -> x0, local copies, waits for them, and re-layouts: 2.54 us -> none  [sent_to_all(): copies = jnp.broadcast_to(array, (lax.axis_size(axis), *array.shape))]
  transfers between devices with their start and end apart: 4 -> 0, of which waited for: 4 -> 0; matrix products, arithmetic and copies ran while one was open for 5% -> 0% of each run, Pallas kernels for 0% -> 0%
where the time goes in v2:
time: 149 us
  Pallas kernels  143 us (96%)
  local copies, waits for them, and re-layouts  4.71 us (3%)
    pallas_call x1, Pallas kernels, shards(): pl.pallas_call(step_kernel, out_shape=(jax.ShapeDtypeStruct((128, 1024),...  143 us
    unnamed x3, local copies, waits for them, and re-layouts  4.71 us

profile of v2, /device:TPU:8, one launch (start us, length us, event | category | flops | bytes accessed | tf_op | source)
XLA Modules:
  0.0 148.7 jit_solution(472012283183426346)
XLA Ops:
  0.6 143.3 %train_step.1 = (bf16[128,1024]{1,0:T(8,128)(2,1)}, bf16[128,1024]{1,0:T(8,128)(2,1)}, f32[2,16,256]{2,1,0:T(8,128)}) custom-call(bf16[128,1024]{1,0:T(8,128)(2,1)} %features.1, s32[1,128]{1,0:T(1,128)} %bitcast.14, s32[1,128]{1,0:T(1,128)} %bitcast.15, s32[1,512]{1,0:T(1,128)} %documents.1, bf16[128,1024]{1,0:T(8,128)(2,1)} %bitcast.12, ...), custom_call_target="tpu_custom_call" | custom-call | tf_op jit(solution)/shard_map/train_step/pallas_call | solution.py:809
  144.0 1.7 %copy.16 = bf16[1,128,1024]{2,1,0:T(8,128)(2,1)} copy(bf16[1,128,1024]{2,1,0:T(8,128)(2,1)} %bitcast.13) | data formatting | bytes 524288
  145.6 1.7 %copy.17 = bf16[128,1024]{1,0:T(8,128)(2,1)} copy(bf16[128,1024]{1,0:T(8,128)(2,1)} %get-tuple-element.13) | data formatting | bytes 524288
  147.3 1.4 copy.18

commit v3 on v2

--- a/solution.py
+++ b/solution.py
@@ -217,19 +217,23 @@
     def along_z(self, shift):
         return (self.event, lax.rem(self.pack + shift + 8, 8), self.tensor)
 
-    def to_pair(self, region):
-        self.pair_started.append(self.copy(region, region, self.partner))
+    def to_pair(self, region, name):
+        self.pair_started.append((name, self.copy(region, region, self.partner)))
+
+    def await_pair(self, names):
+        for name, copy in self.pair_started:
+            if name in names:
+                copy.wait_recv()
 
     def end(self):
         for copy in self.started:
             copy.wait_send()
-        for copy in self.pair_started:
-            copy.wait_recv()
 
 
 class TensorRing:
-    def __init__(self, gather, own, region, halves):
-        self.gather, self.own, self.region, self.halves = gather, own, region, halves
+    def __init__(self, gather, name, own, region, halves):
+        self.gather, self.name, self.own = gather, name, own
+        self.region, self.halves = region, halves
 
     def start(self):
         device = self.gather.along_tensor
@@ -243,8 +247,10 @@
             copy.wait_recv()
         device = self.gather.along_tensor
         plus, minus = self.halves
-        self.far = [self.gather.copy(self.region(2, plus), self.region(3, plus), device(1))]
-        if minus is not None:
+        self.far = []
+        if plus is not False:
+            self.far.append(self.gather.copy(self.region(2, plus), self.region(3, plus), device(1)))
+        if minus is not False:
             self.far.append(
                 self.gather.copy(self.region(1, minus), self.region(3, minus), device(-1))
             )
@@ -252,12 +258,12 @@
     def end(self):
         for copy in self.far:
             copy.wait_recv()
-        self.gather.to_pair(self.region(pl.ds(1, 3)))
+        self.gather.to_pair(self.region(pl.ds(1, 3)), self.name)
 
 
 class SideRing:
-    def __init__(self, gather, size, index, device, region, halves):
-        self.gather, self.size, self.index = gather, size, index
+    def __init__(self, gather, name, size, index, device, region, halves):
+        self.gather, self.name, self.size, self.index = gather, name, size, index
         self.device, self.region, self.halves = device, region, halves
         self.step = 0
         self.flying = None
@@ -286,9 +292,9 @@
                     block = self.block(-sign * step, half)
                     forward.append(self.gather.copy(block, block, self.device(sign)))
             for sign in (1, -1):
-                self.gather.to_pair(self.block(-sign * step))
+                self.gather.to_pair(self.block(-sign * step), self.name)
         else:
-            self.gather.to_pair(self.block(step))
+            self.gather.to_pair(self.block(step), self.name)
         self.flying = forward
         self.step = step + 1
 
@@ -332,18 +338,24 @@
     documents,
     out_grad,
     enc_hbm,
-    attn_in_hbm,
+    first_hbm,
+    second_hbm,
     attn_out_hbm,
-    ffn_in_hbm,
-    ffn_out_hbm,
+    gate_hbm,
+    up_hbm,
+    down_z_hbm,
+    down_t_hbm,
     packed_out,
     row_grad,
     enc_grad,
     enc,
-    attn_in,
+    first,
+    second,
     attn_out,
-    ffn_in,
-    ffn_out,
+    gate_in,
+    up_in,
+    down_z,
+    down_t,
     preact,
     wide,
     send_rows,
@@ -377,6 +389,8 @@
     normed2,
     allowed_ref,
     root_ref,
+    d_proj,
+    gated,
     halo_send,
     halo_got,
     load_sem,
@@ -405,10 +419,13 @@
         (
             (enc_hbm.at[0], enc.at[0]),
             (enc_hbm.at[1], enc.at[1]),
-            (attn_in_hbm, attn_in.at[0]),
+            (first_hbm.at[pl.ds(0, 2)], first.at[0]),
+            (second_hbm.at[pl.ds(2, 2)], second.at[0]),
             (attn_out_hbm, attn_out.at[0]),
-            (ffn_in_hbm, ffn_in.at[0]),
-            (ffn_out_hbm, ffn_out.at[0]),
+            (gate_hbm.at[0], gate_in.at[0]),
+            (up_hbm.at[1], up_in.at[0]),
+            (down_z_hbm.at[0], down_z.at[0]),
+            (down_t_hbm.at[1], down_t.at[0]),
         )
     ):
         load = pltpu.make_async_copy(source, target, load_sem.at[number])
@@ -435,6 +452,9 @@
         value = jnp.sum(jnp.where(picks[k], slot_row, 0.0), axis=1, keepdims=True) - 1.0
         slots = jnp.where(lane == k, value, slots)
     send_slots[:, 0, :] = slots
+    for k in range(CAP):
+        spread_rows(wide, k, dot32(one_hot(picks[k]), features[...]))
+    send_rows[...] = wide[...].astype(bf16).reshape(GROUPS, BLOCK_ROWS, 128)
     pl.semaphore_wait(barrier, 16)
     for step in range(1, 8):
         pl.semaphore_signal(
@@ -445,68 +465,97 @@
         )
 
     gather = Gather(gather_send, gather_recv, event, pack, tensor)
-    both = (pl.ds(0, 2), pl.ds(2, 2))
-
-    def part_a(where, half=None):
-        return attn_in.at[where, slice(None) if half is None else half, chip_x, core]
-
-    def part_o(where, half=None):
-        return attn_out.at[where, pack, core]
-
-    def part_i(where, half=None):
-        return ffn_in.at[where, slice(None) if half is None else half, core]
-
-    def part_f(where, half=None):
-        return ffn_out.at[where, pack, core, slice(None) if half is None else half]
-
-    ring_f = TensorRing(gather, ffn_out_hbm.at[pack, core], part_f, (pl.ds(0, 1), pl.ds(1, 1)))
-    ring_o = TensorRing(gather, attn_out_hbm.at[pack, core], part_o, (None, None))
-    ring_a = TensorRing(gather, attn_in_hbm.at[:, chip_x, core], part_a, both)
-    ring_i = TensorRing(gather, ffn_in_hbm.at[:, core], part_i, (pl.ds(0, 1), pl.ds(1, 1)))
+    whole = slice(None)
+    low, high = pl.ds(0, 1), pl.ds(1, 1)
     foreign = pl.ds(1, 3)
 
-    def side_a(index, half=None):
-        return attn_in.at[foreign, slice(None) if half is None else half, index, core]
-
-    def side_o(index, half=None):
-        return attn_out.at[foreign, index, core]
-
-    def side_f(index, half=None):
-        return ffn_out.at[foreign, index, core, slice(None) if half is None else half]
-
-    x_a = SideRing(gather, 4, chip_x, gather.along_x, side_a, both)
-    z_o = SideRing(gather, 8, pack, gather.along_z, side_o, (None, False))
-    z_f = SideRing(gather, 8, pack, gather.along_z, side_f, (pl.ds(0, 1), pl.ds(1, 1)))
-
-    ring_f.start()
-    ring_o.start()
-    loads[0].wait()
-    acts[0, 0] = features[...]
-    pre = dot32(features[...], enc[0])
-    preact[...] = pre
-    act = silu(pre).astype(bf16)
-    acts[1, 0] = act
-    ring_f.relay()
-    ring_o.relay()
-    ring_a.start()
-    loads[1].wait()
-    encoded = dot32(act, enc[1]).astype(bf16)
-    ring_f.end()
-    ring_o.end()
-    z_f.start()
-    z_o.start()
-    for k in range(CAP):
-        spread_rows(wide, k, dot32(one_hot(picks[k]), encoded))
-    send_rows[...] = wide[...].astype(bf16).reshape(GROUPS, BLOCK_ROWS, 128)
+    def part_of(half):
+        return whole if half is None else half
+
+    def first_at(where, index, half=None):
+        return first.at[where, part_of(half), index, core]
+
+    def second_at(where, index, half=None):
+        return second.at[where, part_of(half), index, core]
+
+    def attn_out_at(where, index, half=None):
+        return attn_out.at[where, index, core, part_of(half)]
+
+    def gate_at(where, index, half=None):
+        return gate_in.at[where, index, core, part_of(half)]
+
+    def down_z_at(where, index, half=None):
+        return down_z.at[where, index, core]
+
+    def up_at(where, half=None):
+        return up_in.at[where, core, part_of(half)]
+
+    def down_t_at(where, half=None):
+        return down_t.at[where, core, part_of(half)]
+
+    def slice_ring(name, own, region, index, halves):
+        return TensorRing(
+            gather, name, own, lambda where, half=None: region(where, index, half), halves
+        )
+
+    t_first = slice_ring(
+        "attn", first_hbm.at[pl.ds(0, 2), chip_x, core], first_at, chip_x, (low, high)
+    )
+    t_second = slice_ring(
+        "attn", second_hbm.at[pl.ds(2, 2), pack, core], second_at, pack, (low, high)
+    )
+    t_out = slice_ring("out", attn_out_hbm.at[chip_x, core], attn_out_at, chip_x, (low, high))
+    t_gate = slice_ring("ffn", gate_hbm.at[0, chip_x, core], gate_at, chip_x, (low, high))
+    t_down = slice_ring("ffn", down_z_hbm.at[0, pack, core], down_z_at, pack, (False, None))
+    t_up = TensorRing(gather, "ffn", up_hbm.at[1, core], up_at, (low, high))
+    t_last = TensorRing(gather, "ffn", down_t_hbm.at[1, core], down_t_at, (low, high))
+
+    def side_ring(name, axis, region, halves):
+        size, index, device = (
+            (4, chip_x, gather.along_x) if axis == "x" else (8, pack, gather.along_z)
+        )
+        return SideRing(
+            gather,
+            name,
+            size,
+            index,
+            device,
+            lambda number, half=None: region(foreign, number, half),
+            halves,
+        )
+
+    x_first = side_ring("attn", "x", first_at, (low, high))
+    z_second = side_ring("attn", "z", second_at, (low, high))
+    x_out = side_ring("out", "x", attn_out_at, (low, high))
+    x_gate = side_ring("ffn", "x", gate_at, (low, high))
+    z_down = side_ring("ffn", "z", down_z_at, (None, False))
+
+    t_second.start()
+    t_first.start()
+    t_down.start()
+    t_out.start()
+    t_gate.start()
     pl.semaphore_wait(ready_sem, 7)
     start_exchange(send_slots, got_slots, me, tensor, send_sem.at[0], recv_sem.at[0])
     start_exchange(send_rows, got_rows, me, tensor, send_sem.at[1], recv_sem.at[1])
-    ring_a.relay()
-    ring_i.start()
-    ring_a.end()
-    x_a.start()
-    z_f.advance()
-    z_o.advance()
+    t_second.relay()
+    t_first.relay()
+    t_down.relay()
+    t_out.relay()
+    t_gate.relay()
+    t_up.start()
+    t_second.end()
+    z_second.start()
+    t_first.end()
+    x_first.start()
+    t_down.end()
+    z_down.start()
+    t_out.end()
+    x_out.start()
+    t_gate.end()
+    allowed, root = masks(documents, tensor)
+    allowed_ref[...] = allowed
+    root_ref[...] = jnp.broadcast_to(root, (128, 128))
 
     def pair_copy(number, array):
         return pltpu.make_async_remote_copy(
@@ -518,9 +567,6 @@
             device_id_type=MESH,
         )
 
-    act_copies = [pair_copy(layer, acts.at[layer]) for layer in range(2)]
-    for copy in act_copies:
-        copy.start()
     end_exchange(send_slots, got_slots, send_sem.at[0], recv_sem.at[0])
     end_exchange(send_rows, got_rows, send_sem.at[1], recv_sem.at[1])
     wide[...] = got_rows[...].reshape(GROUPS * BLOCK_ROWS, 128).astype(f32)
@@ -531,7 +577,13 @@
         pick = one_hot(turned[k : k + 1, :GROUPS] == place)
         term = dot32(pick, joined_rows(wide, k))
         total = term if total is None else total + term
-    quarter = total
+    rows = total.astype(bf16)
+    for load in loads[:2]:
+        load.wait()
+    pre = dot32(rows, enc[0])
+    preact[...] = pre
+    act = silu(pre).astype(bf16)
+    quarter = rounded(dot32(act, enc[1]))
     normed_f, factor1 = norm_rows(quarter)
     halo_send[0] = normed_f.astype(bf16)
     normed[1] = normed_f.astype(bf16)
@@ -549,35 +601,43 @@
 
     halo = halo_copy(0, normed.at[0], 1)
     halo.start()
-    allowed, root = masks(documents, tensor)
-    allowed_ref[...] = allowed
-    root_ref[...] = jnp.broadcast_to(root, (128, 128))
-    z_f.advance()
-    z_o.advance()
-    x_a.advance()
-    z_f.advance()
-    z_o.advance()
-    ring_i.relay()
-    z_f.advance()
-    z_o.advance()
-    x_a.advance()
-    ring_i.end()
-    gather.end()
-    for load in loads[2:]:
+    acts[0, 0] = rows
+    acts[1, 0] = act
+    act_copies = [pair_copy(layer, acts.at[layer]) for layer in range(2)]
+    for copy in act_copies:
+        copy.start()
+    t_last.start()
+    z_second.advance()
+    x_first.advance()
+    x_gate.start()
+    z_down.advance()
+    x_out.advance()
+    z_second.advance()
+    t_up.relay()
+    z_down.advance()
+    x_first.advance()
+    z_second.advance()
+    z_down.advance()
+    z_second.advance()
+    t_last.relay()
+    x_gate.advance()
+    gather.await_pair(("attn",))
+    for load in loads[2:4]:
         load.wait()
     halo.wait()
     own_rows = normed[1]
     all_rows = normed[...].reshape(256, 1024)
     total_a[...] = quarter
 
-    def attend(slot_index, carry):
-        def matrix(number):
-            return attn_in[slot_index, number].reshape(1024, 256)
-
-        query_f = rounded(dot32(own_rows, matrix(0)))
-        gate = rounded(dot32(own_rows, matrix(3)))
-        keys_f = rounded(dot32(all_rows, matrix(1)))
-        values_f = rounded(dot32(all_rows, matrix(2)))
+    def matrix(slot_index, number):
+        source = first if number < 2 else second
+        return source[slot_index, number % 2].reshape(1024, 256)
+
+    def attend(slot_index):
+        query_f = rounded(dot32(own_rows, matrix(slot_index, 0)))
+        gate = rounded(dot32(own_rows, matrix(slot_index, 3)))
+        keys_f = rounded(dot32(all_rows, matrix(slot_index, 1)))
+        values_f = rounded(dot32(all_rows, matrix(slot_index, 2)))
         gates[slot_index] = gate
         sides = []
         for ref, value in ((query, query_f), (keys, keys_f), (values, values_f)):
@@ -606,11 +666,20 @@
             parts.append(part)
         result = jnp.concatenate(parts, axis=1) / root_ref[:, 0:1]
         attended[slot_index] = result
-        gated = (result * silu(gate)).astype(bf16)
-        total_a[...] += rounded(dot32(gated, attn_out[slot_index].reshape(256, 1024)))
-        return carry
-
-    lax.fori_loop(0, 4, attend, 0)
+        gated[slot_index] = (result * silu(gate)).astype(bf16)
+
+    attend(0)
+    z_down.advance()
+    attend(1)
+    attend(2)
+    x_out.advance()
+    attend(3)
+    gather.await_pair(("out",))
+    loads[4].wait()
+    for slot_index in range(4):
+        total_a[...] += rounded(
+            dot32(gated[slot_index], attn_out[slot_index].reshape(256, 1024))
+        )
     resid = rounded(total_a[...])
     normed2_f, factor2 = norm_rows(resid)
     normed2[...] = normed2_f.astype(bf16)
@@ -619,21 +688,30 @@
 
     def feed(slot_index, carry):
         rows = normed2[...]
-        gate = dot32(rows, ffn_in[slot_index, 0].reshape(1024, 512))
-        upper = dot32(rows, ffn_in[slot_index, 1].reshape(1024, 512))
+        gate = dot32(rows, gate_in[slot_index].reshape(1024, 512))
+        upper = dot32(rows, up_in[slot_index].reshape(1024, 512))
         sigma = jax.nn.sigmoid(gate)
         active = gate * sigma
-        down = ffn_out[slot_index].reshape(512, 1024)
-        total_a[...] += rounded(dot32((active * upper).astype(bf16), down))
-        d_hidden = dot32(out_grad[...], down, ((1,), (1,)))
+        down = (down_z[slot_index].reshape(256, 1024), down_t[slot_index].reshape(256, 1024))
+        hidden = (active * upper).astype(bf16)
+        total_a[...] += rounded(dot32(hidden[:, :256], down[0]) + dot32(hidden[:, 256:], down[1]))
+        d_hidden = jnp.concatenate(
+            [dot32(out_grad[...], part, ((1,), (1,))) for part in down], axis=1
+        )
         d_gate = (d_hidden * upper * (sigma * (1.0 + gate * (1.0 - sigma)))).astype(bf16)
         d_upper = (d_hidden * active).astype(bf16)
         total_b[...] += rounded(
-            dot32(d_gate, ffn_in[slot_index, 0].reshape(1024, 512), ((1,), (1,)))
-            + dot32(d_upper, ffn_in[slot_index, 1].reshape(1024, 512), ((1,), (1,)))
+            dot32(d_gate, gate_in[slot_index].reshape(1024, 512), ((1,), (1,)))
+            + dot32(d_upper, up_in[slot_index].reshape(1024, 512), ((1,), (1,)))
         )
         return carry
 
+    x_gate.advance()
+    t_up.end()
+    t_last.end()
+    gather.await_pair(("ffn",))
+    for load in loads[5:]:
+        load.wait()
     lax.fori_loop(0, 4, feed, 0)
     packed_out[...] = total_a[...].astype(bf16)
     d_resid = (
@@ -672,14 +750,10 @@
         d_query, d_keys, d_values = (
             jnp.concatenate(parts, axis=1).astype(bf16) for parts in d_parts
         )
-        keys_back = dot32(d_keys, attn_in[slot_index, 1].reshape(1024, 256), ((1,), (1,)))
-        values_back = dot32(d_values, attn_in[slot_index, 2].reshape(1024, 256), ((1,), (1,)))
-        both_back = keys_back + values_back
-        total_b[...] += both_back[:128]
-        total_a[...] += (
-            both_back[128:]
-            + dot32(d_query, attn_in[slot_index, 0].reshape(1024, 256), ((1,), (1,)))
-            + dot32(d_gate, attn_in[slot_index, 3].reshape(1024, 256), ((1,), (1,)))
+        for number, value in enumerate((d_query, d_keys[128:], d_values[128:], d_gate)):
+            d_proj[slot_index, number] = value
+        total_b[...] += dot32(d_keys[:128], matrix(slot_index, 1), ((1,), (1,))) + dot32(
+            d_values[:128], matrix(slot_index, 2), ((1,), (1,))
         )
         return carry
 
@@ -687,35 +761,34 @@
     halo_send[1] = total_b[...].astype(bf16)
     halo_back = halo_copy(1, halo_got, 3)
     halo_back.start()
+
+    def project_back(slot_index, carry):
+        total_a[...] += sum(
+            dot32(d_proj[slot_index, number], matrix(slot_index, number), ((1,), (1,)))
+            for number in range(4)
+        )
+        return carry
+
+    lax.fori_loop(0, 4, project_back, 0)
     halo_back.wait()
     d_normed = total_a[...] + halo_got[...].astype(f32)
     normed_f, factor1 = norm_rows(residual[...])
     d_quarter = (d_resid.astype(f32) + norm_back(d_normed, normed_f, factor1)).astype(bf16)
+    cots[1, 0] = d_quarter
+    cot_copies = [pair_copy(2 + layer, cots.at[layer]) for layer in range(2)]
+    cot_copies[1].start()
     lane = lax.broadcasted_iota(jnp.int32, (GROUPS, 128), 1).astype(jnp.float32)
     for k in range(CAP):
-        pick = one_hot(got_slots[:, 0, k : k + 1] == lane)
-        spread_rows(wide, k, dot32(pick, d_quarter))
-    send_rows[...] = wide[...].astype(jnp.bfloat16).reshape(GROUPS, BLOCK_ROWS, 128)
+        chosen = one_hot(got_slots[:, 0, k : k + 1] == lane)
+        spread_rows(wide, k, dot32(chosen, d_quarter))
+    send_rows[...] = wide[...].astype(bf16).reshape(GROUPS, BLOCK_ROWS, 128)
     start_exchange(send_rows, back_rows, me, tensor, send_sem.at[2], recv_sem.at[2])
-    picks = routing(owner[...].astype(jnp.float32))
+    cots[0, 0] = (
+        dot32(d_quarter, enc[1], ((1,), (1,))) * silu_grad(preact[...])
+    ).astype(bf16)
+    cot_copies[0].start()
     for copy in act_copies:
         copy.wait()
-    end_exchange(send_rows, back_rows, send_sem.at[2], recv_sem.at[2])
-    wide[...] = back_rows[...].reshape(GROUPS * BLOCK_ROWS, 128).astype(jnp.float32)
-    total = None
-    for k in range(CAP):
-        term = dot32(one_hot(picks[k]), joined_rows(wide, k), ((0,), (0,)))
-        total = term if total is None else total + term
-    cotangent = total.astype(jnp.bfloat16)
-    row_grad[...] = cotangent
-    cots[1, 0] = cotangent
-    cot_copies = [pair_copy(2 + layer, cots.at[layer]) for layer in range(2)]
-    cot_copies[1].start()
-    pre = preact[...]
-    sigma = jax.nn.sigmoid(pre)
-    back = dot32(cotangent, enc[1], ((1,), (1,)))
-    cots[0, 0] = (back * (sigma * (1.0 + pre * (1.0 - sigma)))).astype(jnp.bfloat16)
-    cot_copies[0].start()
 
     def tensor_device(index):
         return (event, pack, index)
@@ -782,12 +855,26 @@
         )
         z_copies[-1].start()
     got_z[pack] = send_z[pack]
+    end_exchange(send_rows, back_rows, send_sem.at[2], recv_sem.at[2])
+    wide[...] = back_rows[...].reshape(GROUPS * BLOCK_ROWS, 128).astype(f32)
+    total = None
+    for k in range(CAP):
+        term = dot32(one_hot(picks[k]), joined_rows(wide, k), ((0,), (0,)))
+        total = term if total is None else total + term
+    row_grad[...] = total.astype(bf16)
+    gather.end()
     for copy in z_copies:
         copy.wait()
     total = got_z[0].astype(jnp.float32)
     for source in range(1, 8):
         total = total + got_z[source].astype(jnp.float32)
     enc_grad[...] = total
+
+
+def hand_over(packed_in, row_in, enc_in, packed_out, row_out, enc_out):
+    packed_out[...] = packed_in[...]
+    row_out[...] = row_in[...]
+    enc_out[...] = enc_in[...]
 
 
 def shards(
@@ -813,14 +900,17 @@
             jax.ShapeDtypeStruct((128, 1024), bf16),
             jax.ShapeDtypeStruct((2, 16, 256), f32),
         ),
-        in_specs=[vmem] * 5 + [hbm] * 5,
+        in_specs=[vmem] * 5 + [hbm] * 8,
         out_specs=(vmem, vmem, vmem),
         scratch_shapes=[
             pltpu.VMEM((2, 1024, 1024), bf16),
-            pltpu.VMEM((4, 4, 4, 2, 128, 256), bf16),
+            pltpu.VMEM((4, 2, 4, 2, 128, 256), bf16),
+            pltpu.VMEM((4, 2, 8, 2, 64, 256), bf16),
+            pltpu.VMEM((4, 4, 2, 2, 16, 1024), bf16),
+            pltpu.VMEM((4, 4, 2, 2, 64, 512), bf16),
+            pltpu.VMEM((4, 2, 2, 256, 512), bf16),
             pltpu.VMEM((4, 8, 2, 16, 1024), bf16),
-            pltpu.VMEM((4, 2, 2, 512, 512), bf16),
-            pltpu.VMEM((4, 8, 2, 2, 16, 1024), bf16),
+            pltpu.VMEM((4, 2, 2, 64, 1024), bf16),
             pltpu.VMEM((128, 1024), f32),
             pltpu.VMEM((GROUPS * BLOCK_ROWS, 128), f32),
             pltpu.VMEM((GROUPS, BLOCK_ROWS, 128), bf16),
@@ -854,14 +944,16 @@
             pltpu.VMEM((128, 1024), bf16),
             pltpu.VMEM((128, 256), f32),
             pltpu.VMEM((128, 128), f32),
+            pltpu.VMEM((4, 4, 128, 256), bf16),
+            pltpu.VMEM((4, 128, 256), bf16),
             pltpu.VMEM((2, 128, 1024), bf16),
             pltpu.VMEM((128, 1024), bf16),
-            dma((6,)),
+            dma((9,)),
             dma((3,)),
             dma((3,)),
             pltpu.SemaphoreType.REGULAR,
-            dma((64,)),
-            dma((64,)),
+            dma((96,)),
+            dma((96,)),
             dma((4,)),
             dma((4,)),
             dma((24,)),
@@ -882,10 +974,24 @@
         out_grad[0],
         enc_weight,
         attn_in.reshape(4, 4, 2, 128, 256),
-        attn_out.reshape(8, 2, 16, 1024),
-        ffn_in.reshape(2, 2, 512, 512),
-        ffn_out.reshape(8, 2, 2, 16, 1024),
+        attn_in.reshape(4, 8, 2, 64, 256),
+        attn_out.reshape(4, 2, 2, 16, 1024),
+        ffn_in.reshape(2, 4, 2, 2, 64, 512),
+        ffn_in.reshape(2, 2, 2, 256, 512),
+        ffn_out.reshape(2, 8, 2, 16, 1024),
+        ffn_out.reshape(2, 2, 2, 64, 1024),
     )
+    packed_out, row_grad, enc_grad = pl.pallas_call(
+        hand_over,
+        out_shape=(
+            jax.ShapeDtypeStruct((128, 1024), bf16),
+            jax.ShapeDtypeStruct((128, 1024), bf16),
+            jax.ShapeDtypeStruct((2, 16, 256), f32),
+        ),
+        in_specs=[vmem] * 3,
+        out_specs=(vmem, vmem, vmem),
+        name="hand_over",
+    )(packed_out, row_grad, enc_grad)
     return (packed_out[None], row_grad, enc_grad)
 
 

time: 149 us -> 125 us (0.84)
  Pallas kernels: 143 us -> 124 us
  local copies, waits for them, and re-layouts: 4.71 us -> 0 us
    pallas_call x1, Pallas kernels: 143 us -> 122 us  [shards(): pl.pallas_call(step_kernel, out_shape=(jax.ShapeDtypeStruct((128, 1024),...]
    unnamed x3 -> x0, local copies, waits for them, and re-layouts: 4.71 us -> none
    pallas_call x0 -> x1, Pallas kernels: none -> 1.84 us  [shards(): pl.pallas_call(hand_over, out_shape=(jax.ShapeDtypeStruct((128, 1024), bf...]
where the time goes in v3:
time: 125 us
  Pallas kernels  124 us (99%)
    pallas_call x1, Pallas kernels, shards(): pl.pallas_call(step_kernel, out_shape=(jax.ShapeDtypeStruct((128, 1024),...  122 us

profile of v3, /device:TPU:8, one launch (start us, length us, event | category | flops | bytes accessed | tf_op | source)
XLA Modules:
  0.0 124.7 jit_solution(9126331760167481343)
XLA Ops:
  0.6 122.2 %train_step.1 = (bf16[128,1024]{1,0:T(8,128)(2,1)}, bf16[128,1024]{1,0:T(8,128)(2,1)}, f32[2,16,256]{2,1,0:T(8,128)}) custom-call(bf16[128,1024]{1,0:T(8,128)(2,1)} %features.1, s32[1,128]{1,0:T(1,128)} %bitcast.19, s32[1,128]{1,0:T(1,128)} %bitcast.20, s32[1,512]{1,0:T(1,128)} %documents.1, bf16[128,1024]{1,0:T(8,128)(2,1)} %bitcast.18, ...), custom_call_target="tpu_custom_call" | custom-call | tf_op jit(solution)/shard_map/train_step/pallas_call | solution.py:896
  122.9 1.8 %hand_over.1 = (bf16[128,1024]{1,0:T(8,128)(2,1)}, bf16[128,1024]{1,0:T(8,128)(2,1)}, f32[2,16,256]{2,1,0:T(8,128)}) custom-call(bf16[128,1024]{1,0:T(8,128)(2,1)} %get-tuple-element.9.packed_in, bf16[128,1024]{1,0:T(8,128)(2,1)} %get-tuple-element.10.row_in, f32[2,16,256]{2,1,0:T(8,128)} %get-tuple-element.11.enc_in), custom_call_target="tpu_custom_call" | custom-call | tf_op jit(solution)/shard_map/hand_over/pallas_call | solution.py:984

commit v4 on v3

--- a/solution.py
+++ b/solution.py
@@ -32,39 +32,27 @@
     return (lax.axis_index("event"), lax.axis_index("pack"), lax.axis_index("tensor"))
 
 
-def peer(index, tensor):
-    return (index // 8, lax.rem(index, 8), tensor)
-
-
-def greet_all(barrier, me, tensor):
-    def greet(step, carry):
-        pl.semaphore_signal(
-            barrier, inc=1, device_id=peer(lax.rem(me + step, GROUPS), tensor), device_id_type=MESH
-        )
+def start_exchange(source, target, event, pack, tensor, send_sem, recv_sem, first=1, last=GROUPS):
+    me = event * 8 + pack
+
+    def start(step, carry):
+        chip = lax.rem(event // 2 + step // 16, 4)
+        core = lax.rem(event + step // 8, 2)
+        other_pack = lax.rem(pack + step, 8)
+        other_event = chip * 2 + core
+        pltpu.make_async_remote_copy(
+            src_ref=source.at[other_event * 8 + other_pack],
+            dst_ref=target.at[me],
+            send_sem=send_sem,
+            recv_sem=recv_sem,
+            device_id=(other_event, other_pack, tensor),
+            device_id_type=MESH,
+        ).start()
         return carry
 
-    lax.fori_loop(1, GROUPS, greet, 0)
-
-
-def exchange_copy(source, target, me, tensor, step, send_sem, recv_sem):
-    other = lax.rem(me + step, GROUPS)
-    return pltpu.make_async_remote_copy(
-        src_ref=source.at[other],
-        dst_ref=target.at[me],
-        send_sem=send_sem,
-        recv_sem=recv_sem,
-        device_id=peer(other, tensor),
-        device_id_type=MESH,
-    )
-
-
-def start_exchange(source, target, me, tensor, send_sem, recv_sem):
-    def start(step, carry):
-        exchange_copy(source, target, me, tensor, step, send_sem, recv_sem).start()
-        return carry
-
-    lax.fori_loop(1, GROUPS, start, 0)
-    target[me] = source[me]
+    lax.fori_loop(first, last, start, 0)
+    if first == 1:
+        target[me] = source[me]
 
 
 def await_bytes(ref, sem):
@@ -254,11 +242,12 @@
             self.far.append(
                 self.gather.copy(self.region(1, minus), self.region(3, minus), device(-1))
             )
+        self.gather.to_pair(self.region(pl.ds(1, 2)), self.name)
 
     def end(self):
         for copy in self.far:
             copy.wait_recv()
-        self.gather.to_pair(self.region(pl.ds(1, 3)), self.name)
+        self.gather.to_pair(self.region(pl.ds(3, 1)), self.name)
 
 
 class SideRing:
@@ -345,9 +334,11 @@
     up_hbm,
     down_z_hbm,
     down_t_hbm,
+    packed_hbm,
+    row_hbm,
+    enc_grad,
     packed_out,
     row_grad,
-    enc_grad,
     enc,
     first,
     second,
@@ -383,6 +374,7 @@
     attended,
     weights,
     slopes,
+    slopes16,
     total_a,
     total_b,
     residual,
@@ -408,7 +400,6 @@
     halo_sem,
 ):
     event, pack, tensor = where_am_i()
-    me = event * 8 + pack
     core = lax.rem(event, 2)
     chip_x = event // 2
     partner = (event + 1 - 2 * core, pack, tensor)
@@ -536,23 +527,18 @@
     t_out.start()
     t_gate.start()
     pl.semaphore_wait(ready_sem, 7)
-    start_exchange(send_slots, got_slots, me, tensor, send_sem.at[0], recv_sem.at[0])
-    start_exchange(send_rows, got_rows, me, tensor, send_sem.at[1], recv_sem.at[1])
+    start_exchange(send_slots, got_slots, event, pack, tensor, send_sem.at[0], recv_sem.at[0])
+    start_exchange(send_rows, got_rows, event, pack, tensor, send_sem.at[1], recv_sem.at[1])
     t_second.relay()
     t_first.relay()
+    t_up.start()
     t_down.relay()
-    t_out.relay()
-    t_gate.relay()
-    t_up.start()
     t_second.end()
     z_second.start()
+    t_out.relay()
     t_first.end()
     x_first.start()
-    t_down.end()
-    z_down.start()
-    t_out.end()
-    x_out.start()
-    t_gate.end()
+    t_gate.relay()
     allowed, root = masks(documents, tensor)
     allowed_ref[...] = allowed
     root_ref[...] = jnp.broadcast_to(root, (128, 128))
@@ -609,19 +595,17 @@
     t_last.start()
     z_second.advance()
     x_first.advance()
+    t_down.end()
+    z_down.start()
+    t_out.end()
+    x_out.start()
+    z_second.advance()
+    t_gate.end()
     x_gate.start()
-    z_down.advance()
-    x_out.advance()
-    z_second.advance()
     t_up.relay()
-    z_down.advance()
     x_first.advance()
     z_second.advance()
     z_down.advance()
-    z_second.advance()
-    t_last.relay()
-    x_gate.advance()
-    gather.await_pair(("attn",))
     for load in loads[2:4]:
         load.wait()
     halo.wait()
@@ -669,9 +653,15 @@
         gated[slot_index] = (result * silu(gate)).astype(bf16)
 
     attend(0)
+    z_second.advance()
+    gather.await_pair(("attn",))
+    x_out.advance()
     z_down.advance()
     attend(1)
+    x_gate.advance()
+    t_last.relay()
     attend(2)
+    z_down.advance()
     x_out.advance()
     attend(3)
     gather.await_pair(("out",))
@@ -706,6 +696,7 @@
         )
         return carry
 
+    z_down.advance()
     x_gate.advance()
     t_up.end()
     t_last.end()
@@ -714,6 +705,11 @@
         load.wait()
     lax.fori_loop(0, 4, feed, 0)
     packed_out[...] = total_a[...].astype(bf16)
+    stores = [
+        pltpu.make_async_copy(packed_out, packed_hbm, load_sem.at[0]),
+        pltpu.make_async_copy(row_grad, row_hbm, load_sem.at[1]),
+    ]
+    stores[0].start()
     d_resid = (
         out_grad[...].astype(f32) + norm_back(total_b[...], normed2_f, factor2)
     ).astype(bf16)
@@ -728,29 +724,28 @@
         d_gate = (
             d_gated * attended[slot_index] * (sigma * (1.0 + gate * (1.0 - sigma)))
         ).astype(bf16)
-        d_parts = [[], [], []]
+        d_parts = [[], []]
         for pair in range(2):
             columns = slice(pair * 128, (pair + 1) * 128)
-            sums = [None, None, None]
+            sums = [None, None]
             for parity in range(2):
                 head = pair * 2 + parity
                 d_side = d_attended[parity][:, columns]
                 d_weights = dot32(d_side, values[slot_index, parity, :, columns], ((1,), (1,)))
                 d_scores = (d_weights * slopes[slot_index, head]).astype(bf16)
+                slopes16[slot_index, head] = d_scores
                 terms = (
-                    dot32(d_scores, keys[slot_index, parity, :, columns]),
                     dot32(d_scores, query[slot_index, parity, :, columns], ((0,), (0,))),
                     dot32(weights[slot_index, head], d_side, ((0,), (0,))),
                 )
                 for number, term in enumerate(terms):
                     sums[number] = term if sums[number] is None else sums[number] + term
             d_parts[0].append(sums[0] * HEAD_SCALE)
-            d_parts[1].append(sums[1] * HEAD_SCALE)
-            d_parts[2].append(sums[2])
-        d_query, d_keys, d_values = (
+            d_parts[1].append(sums[1])
+        d_keys, d_values = (
             jnp.concatenate(parts, axis=1).astype(bf16) for parts in d_parts
         )
-        for number, value in enumerate((d_query, d_keys[128:], d_values[128:], d_gate)):
+        for number, value in enumerate((d_keys[128:], d_values[128:], d_gate)):
             d_proj[slot_index, number] = value
         total_b[...] += dot32(d_keys[:128], matrix(slot_index, 1), ((1,), (1,))) + dot32(
             d_values[:128], matrix(slot_index, 2), ((1,), (1,))
@@ -763,9 +758,20 @@
     halo_back.start()
 
     def project_back(slot_index, carry):
-        total_a[...] += sum(
-            dot32(d_proj[slot_index, number], matrix(slot_index, number), ((1,), (1,)))
-            for number in range(4)
+        parts = []
+        for pair in range(2):
+            columns = slice(pair * 128, (pair + 1) * 128)
+            parts.append(
+                (
+                    dot32(slopes16[slot_index, pair * 2], keys[slot_index, 0, :, columns])
+                    + dot32(slopes16[slot_index, pair * 2 + 1], keys[slot_index, 1, :, columns])
+                )
+                * HEAD_SCALE
+            )
+        d_query = jnp.concatenate(parts, axis=1).astype(bf16)
+        total_a[...] += dot32(d_query, matrix(slot_index, 0), ((1,), (1,))) + sum(
+            dot32(d_proj[slot_index, number - 1], matrix(slot_index, number), ((1,), (1,)))
+            for number in range(1, 4)
         )
         return carry
 
@@ -777,12 +783,6 @@
     cots[1, 0] = d_quarter
     cot_copies = [pair_copy(2 + layer, cots.at[layer]) for layer in range(2)]
     cot_copies[1].start()
-    lane = lax.broadcasted_iota(jnp.int32, (GROUPS, 128), 1).astype(jnp.float32)
-    for k in range(CAP):
-        chosen = one_hot(got_slots[:, 0, k : k + 1] == lane)
-        spread_rows(wide, k, dot32(chosen, d_quarter))
-    send_rows[...] = wide[...].astype(bf16).reshape(GROUPS, BLOCK_ROWS, 128)
-    start_exchange(send_rows, back_rows, me, tensor, send_sem.at[2], recv_sem.at[2])
     cots[0, 0] = (
         dot32(d_quarter, enc[1], ((1,), (1,))) * silu_grad(preact[...])
     ).astype(bf16)
@@ -796,18 +796,18 @@
     def chip_device(index):
         return (index * 2 + core, pack, tensor)
 
-    rings = ((chip_x, chip_device), (tensor, tensor_device))
+    rings = ((tensor, tensor_device), (chip_x, chip_device))
     stages = [[], []]
-    for layer in range(2):
+    for unit in range(4):
         for stage, refs in enumerate(
             ((grads, firsts, seconds, outs), (grads2, firsts2, seconds2, outs2))
         ):
-            index, device = rings[layer] if stage == 0 else rings[1 - layer]
+            index, device = rings[stage if unit < 3 else 1 - stage]
             stages[stage].append(
                 Halving(
-                    *(ref.at[layer] for ref in refs),
+                    *(ref.at[unit] for ref in refs),
                     (half_send, half_recv),
-                    (stage * 2 + layer) * 6,
+                    (stage * 4 + unit) * 6,
                     index,
                     device,
                 )
@@ -815,31 +815,43 @@
     for layer in (1, 0):
         cot_copies[layer].wait()
         cot = cots[layer].reshape(256, 1024)
+        units = (0, 1) if layer == 1 else (2, 3)
         for chip in range(4):
             columns = pl.ds(pl.multiple_of((chip * 2 + core) * 128, 128), 128)
             act = acts[layer, :, :, columns].reshape(256, 128)
-            term = dot32(act, cot, ((0,), (0,))).astype(jnp.bfloat16)
+            term = dot32(act, cot, ((0,), (0,))).astype(bf16)
             for block in range(4):
                 for half in range(2):
-                    piece = term[half * 64 : (half + 1) * 64, block * 256 : (block + 1) * 256]
-                    if layer == 1:
-                        grads[layer, block, half, chip] = piece
-                    else:
-                        grads[layer, chip, half, block] = piece
-        stages[0][layer].start_one()
-    for layer in (1, 0):
-        stages[0][layer].start_two()
-    for layer in (1, 0):
-        for half, value in enumerate(stages[0][layer].finish()):
+                    for part in range(2):
+                        low_row = half * 64 + part * 32
+                        piece = term[low_row : low_row + 32, block * 256 : (block + 1) * 256]
+                        if units[part] < 3:
+                            grads[units[part], block, half, chip] = piece
+                        else:
+                            grads[units[part], chip, half, block] = piece
+        for unit in units:
+            stages[0][unit].start_one()
+    lane = lax.broadcasted_iota(jnp.int32, (GROUPS, 128), 1).astype(jnp.float32)
+    for k in range(CAP):
+        chosen = one_hot(got_slots[:, 0, k : k + 1] == lane)
+        spread_rows(wide, k, dot32(chosen, d_quarter))
+    send_rows[...] = wide[...].astype(bf16).reshape(GROUPS, BLOCK_ROWS, 128)
+    start_exchange(send_rows, back_rows, event, pack, tensor, send_sem.at[2], recv_sem.at[2])
+    for unit in range(4):
+        stages[0][unit].start_two()
+    for unit in range(4):
+        for half, value in enumerate(stages[0][unit].finish()):
             for block in range(4):
-                grads2[layer, block, half] = value[block]
-        stages[1][layer].start_one()
-    for layer in (1, 0):
-        stages[1][layer].start_two()
-    for layer in (1, 0):
-        for half, value in enumerate(stages[1][layer].finish()):
-            for quarter in range(4):
-                send_z[half * 4 + quarter, layer] = value[quarter * 16 : (quarter + 1) * 16]
+                grads2[unit, block, half] = value[block]
+        stages[1][unit].start_one()
+    for unit in range(4):
+        stages[1][unit].start_two()
+    for unit in range(4):
+        for half, value in enumerate(stages[1][unit].finish()):
+            for number in range(2):
+                send_z[half * 4 + unit % 2 * 2 + number, 1 - unit // 2] = value[
+                    number * 16 : (number + 1) * 16
+                ]
     z_copies = []
     for step in (1, 7, 2, 6, 3, 5, 4):
         other = lax.rem(pack + step, 8)
@@ -862,6 +874,7 @@
         term = dot32(one_hot(picks[k]), joined_rows(wide, k), ((0,), (0,)))
         total = term if total is None else total + term
     row_grad[...] = total.astype(bf16)
+    stores[1].start()
     gather.end()
     for copy in z_copies:
         copy.wait()
@@ -869,6 +882,8 @@
     for source in range(1, 8):
         total = total + got_z[source].astype(jnp.float32)
     enc_grad[...] = total
+    for store in stores:
+        store.wait()
 
 
 def hand_over(packed_in, row_in, enc_in, packed_out, row_out, enc_out):
@@ -901,8 +916,10 @@
             jax.ShapeDtypeStruct((2, 16, 256), f32),
         ),
         in_specs=[vmem] * 5 + [hbm] * 8,
-        out_specs=(vmem, vmem, vmem),
+        out_specs=(hbm, hbm, vmem),
         scratch_shapes=[
+            pltpu.VMEM((128, 1024), bf16),
+            pltpu.VMEM((128, 1024), bf16),
             pltpu.VMEM((2, 1024, 1024), bf16),
             pltpu.VMEM((4, 2, 4, 2, 128, 256), bf16),
             pltpu.VMEM((4, 2, 8, 2, 64, 256), bf16),
@@ -920,14 +937,14 @@
             pltpu.VMEM((GROUPS, BLOCK_ROWS, 128), bf16),
             pltpu.VMEM((2, 2, 128, 1024), bf16),
             pltpu.VMEM((2, 2, 128, 1024), bf16),
-            pltpu.VMEM((2, 4, 2, 4, 64, 256), bf16),
-            pltpu.VMEM((2, 2, 2, 4, 64, 256), bf16),
-            pltpu.VMEM((2, 2, 4, 64, 256), bf16),
-            pltpu.VMEM((2, 2, 4, 64, 256), bf16),
-            pltpu.VMEM((2, 4, 2, 64, 256), bf16),
-            pltpu.VMEM((2, 2, 2, 64, 256), bf16),
-            pltpu.VMEM((2, 2, 64, 256), bf16),
-            pltpu.VMEM((2, 2, 64, 256), bf16),
+            pltpu.VMEM((4, 4, 2, 4, 32, 256), bf16),
+            pltpu.VMEM((4, 2, 2, 4, 32, 256), bf16),
+            pltpu.VMEM((4, 2, 4, 32, 256), bf16),
+            pltpu.VMEM((4, 2, 4, 32, 256), bf16),
+            pltpu.VMEM((4, 4, 2, 32, 256), bf16),
+            pltpu.VMEM((4, 2, 2, 32, 256), bf16),
+            pltpu.VMEM((4, 2, 32, 256), bf16),
+            pltpu.VMEM((4, 2, 32, 256), bf16),
             pltpu.VMEM((8, 2, 16, 256), bf16),
             pltpu.VMEM((8, 2, 16, 256), bf16),
             pltpu.VMEM((2, 128, 1024), bf16),
@@ -938,13 +955,14 @@
             pltpu.VMEM((4, 128, 256), f32),
             pltpu.VMEM((4, 4, 128, 256), bf16),
             pltpu.VMEM((4, 4, 128, 256), f32),
+            pltpu.VMEM((4, 4, 128, 256), bf16),
             pltpu.VMEM((128, 1024), f32),
             pltpu.VMEM((128, 1024), f32),
             pltpu.VMEM((128, 1024), f32),
             pltpu.VMEM((128, 1024), bf16),
             pltpu.VMEM((128, 256), f32),
             pltpu.VMEM((128, 128), f32),
-            pltpu.VMEM((4, 4, 128, 256), bf16),
+            pltpu.VMEM((4, 3, 128, 256), bf16),
             pltpu.VMEM((4, 128, 256), bf16),
             pltpu.VMEM((2, 128, 1024), bf16),
             pltpu.VMEM((128, 1024), bf16),
@@ -956,8 +974,8 @@
             dma((96,)),
             dma((4,)),
             dma((4,)),
-            dma((24,)),
-            dma((24,)),
+            dma((48,)),
+            dma((48,)),
             dma((8,)),
             dma((8,)),
             dma((4,)),

time: 125 us -> 117 us (0.936)
  Pallas kernels: 124 us -> 117 us
    pallas_call x1, Pallas kernels: 122 us -> 115 us  [shards(): pl.pallas_call(step_kernel, out_shape=(jax.ShapeDtypeStruct((128, 1024),...]
where the time goes in v4:
time: 117 us
  Pallas kernels  117 us (100%)
    pallas_call x1, Pallas kernels, shards(): pl.pallas_call(step_kernel, out_shape=(jax.ShapeDtypeStruct((128, 1024),...  115 us

profile of v4, /device:TPU:8, one launch (start us, length us, event | category | flops | bytes accessed | tf_op | source)
XLA Modules:
  0.0 117.2 jit_solution(371194678549553152)
XLA Ops:
  0.6 114.7 %train_step.1 = (bf16[128,1024]{1,0:T(8,128)(2,1)}, bf16[128,1024]{1,0:T(8,128)(2,1)}, f32[2,16,256]{2,1,0:T(8,128)}) custom-call(bf16[128,1024]{1,0:T(8,128)(2,1)} %features.1, s32[1,128]{1,0:T(1,128)} %bitcast.19, s32[1,128]{1,0:T(1,128)} %bitcast.20, s32[1,512]{1,0:T(1,128)} %documents.1, bf16[128,1024]{1,0:T(8,128)(2,1)} %bitcast.18, ...), custom_call_target="tpu_custom_call" | custom-call | tf_op jit(solution)/shard_map/train_step/pallas_call | solution.py:911
  115.3 1.8 %hand_over.1 = (bf16[128,1024]{1,0:T(8,128)(2,1)}, bf16[128,1024]{1,0:T(8,128)(2,1)}, f32[2,16,256]{2,1,0:T(8,128)}) custom-call(bf16[128,1024]{1,0:T(8,128)(2,1)} %get-tuple-element.9.packed_in, bf16[128,1024]{1,0:T(8,128)(2,1)} %get-tuple-element.10.row_in, f32[2,16,256]{2,1,0:T(8,128)} %get-tuple-element.11.enc_in), custom_call_target="tpu_custom_call" | custom-call | tf_op jit(solution)/shard_map/hand_over/pallas_call | solution.py:1002

commit v5 on v4

--- a/solution.py
+++ b/solution.py
@@ -523,22 +523,22 @@
 
     t_second.start()
     t_first.start()
-    t_down.start()
-    t_out.start()
-    t_gate.start()
     pl.semaphore_wait(ready_sem, 7)
     start_exchange(send_slots, got_slots, event, pack, tensor, send_sem.at[0], recv_sem.at[0])
     start_exchange(send_rows, got_rows, event, pack, tensor, send_sem.at[1], recv_sem.at[1])
     t_second.relay()
     t_first.relay()
-    t_up.start()
-    t_down.relay()
+    t_gate.start()
+    t_out.start()
+    t_down.start()
     t_second.end()
     z_second.start()
-    t_out.relay()
     t_first.end()
     x_first.start()
     t_gate.relay()
+    t_out.relay()
+    t_down.relay()
+    t_up.start()
     allowed, root = masks(documents, tensor)
     allowed_ref[...] = allowed
     root_ref[...] = jnp.broadcast_to(root, (128, 128))
@@ -593,16 +593,17 @@
     for copy in act_copies:
         copy.start()
     t_last.start()
-    z_second.advance()
-    x_first.advance()
-    t_down.end()
-    z_down.start()
     t_out.end()
     x_out.start()
     z_second.advance()
     t_gate.end()
+    t_down.end()
+    z_down.start()
+    x_first.advance()
     x_gate.start()
-    t_up.relay()
+    z_second.advance()
+    x_out.advance()
+    z_down.advance()
     x_first.advance()
     z_second.advance()
     z_down.advance()
@@ -653,16 +654,16 @@
         gated[slot_index] = (result * silu(gate)).astype(bf16)
 
     attend(0)
+    t_up.relay()
     z_second.advance()
     gather.await_pair(("attn",))
-    x_out.advance()
+    x_gate.advance()
     z_down.advance()
     attend(1)
-    x_gate.advance()
+    x_out.advance()
+    attend(2)
     t_last.relay()
-    attend(2)
     z_down.advance()
-    x_out.advance()
     attend(3)
     gather.await_pair(("out",))
     loads[4].wait()
@@ -696,14 +697,14 @@
         )
         return carry
 
-    z_down.advance()
+    for load in loads[5:]:
+        load.wait()
+    feed(0, 0)
     x_gate.advance()
     t_up.end()
     t_last.end()
     gather.await_pair(("ffn",))
-    for load in loads[5:]:
-        load.wait()
-    lax.fori_loop(0, 4, feed, 0)
+    lax.fori_loop(1, 4, feed, 0)
     packed_out[...] = total_a[...].astype(bf16)
     stores = [
         pltpu.make_async_copy(packed_out, packed_hbm, load_sem.at[0]),

time: 117 us -> 116 us (level)
  Pallas kernels: 117 us -> 115 us
    pallas_call x1, Pallas kernels: 115 us -> 113 us  [shards(): pl.pallas_call(step_kernel, out_shape=(jax.ShapeDtypeStruct((128, 1024),...]
where the time goes in v5:
time: 116 us
  Pallas kernels  115 us (99%)
    pallas_call x1, Pallas kernels, shards(): pl.pallas_call(step_kernel, out_shape=(jax.ShapeDtypeStruct((128, 1024),...  113 us

profile of v5, /device:TPU:8, one launch (start us, length us, event | category | flops | bytes accessed | tf_op | source)
XLA Modules:
  0.0 115.5 jit_solution(274634533529018284)
XLA Ops:
  0.6 113.1 %train_step.1 = (bf16[128,1024]{1,0:T(8,128)(2,1)}, bf16[128,1024]{1,0:T(8,128)(2,1)}, f32[2,16,256]{2,1,0:T(8,128)}) custom-call(bf16[128,1024]{1,0:T(8,128)(2,1)} %features.1, s32[1,128]{1,0:T(1,128)} %bitcast.19, s32[1,128]{1,0:T(1,128)} %bitcast.20, s32[1,512]{1,0:T(1,128)} %documents.1, bf16[128,1024]{1,0:T(8,128)(2,1)} %bitcast.18, ...), custom_call_target="tpu_custom_call" | custom-call | tf_op jit(solution)/shard_map/train_step/pallas_call | solution.py:912
  113.7 1.8 %hand_over.1 = (bf16[128,1024]{1,0:T(8,128)(2,1)}, bf16[128,1024]{1,0:T(8,128)(2,1)}, f32[2,16,256]{2,1,0:T(8,128)}) custom-call(bf16[128,1024]{1,0:T(8,128)(2,1)} %get-tuple-element.9.packed_in, bf16[128,1024]{1,0:T(8,128)(2,1)} %get-tuple-element.10.row_in, f32[2,16,256]{2,1,0:T(8,128)} %get-tuple-element.11.enc_in), custom_call_target="tpu_custom_call" | custom-call | tf_op jit(solution)/shard_map/hand_over/pallas_call | solution.py:1003
